TPU v7x, 128 devices: a whole 4x4x4 slice. The times are simulated.
128 devices in a mesh: group: 8 (over y, core), rep: 16 (over x, z).
Axes of the slice: x: 4, y: 4, z: 4, core: 2. Of those that a mesh axis runs over, the one named last changes fastest.
Arguments:
- table_hot: bfloat16 [131072, 512], P(('group', 'rep')), may hold values from -6 to 6
- table_mid: bfloat16 [524288, 128], P(('group', 'rep')), may hold values from -6 to 6
- table_cold: bfloat16 [524288, 128], P(('group', 'rep')), may hold values from -6 to 6
- proj_hot: bfloat16 [512, 256], replicated, may hold values from -0.25 to 0.25
- proj_mid: bfloat16 [128, 256], replicated, may hold values from -0.5 to 0.5
- proj_cold: bfloat16 [32, 256], replicated, may hold values from -1 to 1
- tower_in: bfloat16 [256, 1024], replicated, may hold values from -0.375 to 0.375
- tower_out: bfloat16 [1024, 256], replicated, may hold values from -0.1875 to 0.1875
- queries: bfloat16 [65536, 256], P(('group', 'rep')), may hold values from -68 to 68
- labels: int32 [65536], P(('group', 'rep')), may hold values from 0 to 8191
- item_slot: int32 [128, 4, 1024], P(('group', 'rep')), may hold values from 0 to 1023
- item_block: int32 [128, 4, 1024], P(('group', 'rep')), may hold values from 0 to 2
- serve_rows: int32 [128, 3, 1024], P(('group', 'rep')), may hold values from 0 to 16383, as said below
Outputs:
- query_loss: float32 [65536], P(('group', 'rep'))
- query_grad: float32 [65536, 256], P(('group', 'rep'))
- grad_hot: float32 [131072, 512], P(('group', 'rep'))
- grad_mid: float32 [524288, 128], P(('group', 'rep'))
- grad_cold: float32 [524288, 128], P(('group', 'rep'))
- grad_proj_hot: float32 [512, 256], P(None, 'rep')
- grad_proj_mid: float32 [128, 256], P(None, 'rep')
- grad_proj_cold: float32 [32, 256], P(None, 'rep')
- grad_tower_in: float32 [256, 1024], P(None, 'rep')
- grad_tower_out: float32 [1024, 256], P(None, 'rep')
Inputs may be any that keep to these rules, and one draw needn't show every extreme that they name: serve_rows[o, b, d * 8 + c] is a row of owner o's shard of block b that requester d sees in slot c; for block 0 it is below 1024, for block 1 below 4096, for block 2 below 16384; the 8 rows that one owner serves to one requester in one block are distinct.
All inputs are finite; a program needn't handle non-finite values.
Results may differ from a plain program's by a relative error of at most 0.02.
The roundings to bfloat16 on the way count: a program that leaves them out, or rounds other values in their place, can miss the bound.
Values may be sent and summed in bfloat16 or wider, within the bound.
A program may use at most 128 MiB of HBM per device.

v0:
```python
import functools

import jax
import jax.numpy as jnp
from jax import lax
from jax.experimental import pallas as pl
from jax.experimental.pallas import tpu as pltpu
from jax.sharding import PartitionSpec as P

NORM_EPS = 1e-06
LOGIT_SCALE = 0.2
BF = jnp.bfloat16
F32 = jnp.float32
BOTH = ("group", "rep")
MESH = pl.DeviceIdType.MESH
SCALE2 = LOGIT_SCALE * 1.4426950408889634
LN2 = 0.6931471805599453
DMA = pltpu.SemaphoreType.DMA


def mm(a, b):
    return lax.dot_general(a, b, (((1,), (0,)), ((), ())), preferred_element_type=F32)


def mm_nt(a, b):
    return lax.dot_general(a, b, (((1,), (1,)), ((), ())), preferred_element_type=F32)


def mm_tn(a, b):
    return lax.dot_general(a, b, (((0,), (0,)), ((), ())), preferred_element_type=F32)


def flat(block):
    lead = block.shape[0] * block.shape[1]
    return block.astype(F32).reshape(lead, block.shape[2]).astype(BF)


def tiled(value):
    return value.reshape(value.shape[0] // 8, 8, value.shape[1])


def picks(index, shape, axis):
    return jnp.where(index == lax.broadcasted_iota(jnp.int32, shape, axis), 1.0, 0.0)


def step_kernel(
    t_hot, t_mid, t_cold, p_hot, p_mid, p_cold, w_in, w_out, queries, labels, cols, rows,
    back_ref, rows_hot, qg_out, loss_out, fin_ref,
    v_hot, v_mid, v_cold, v_ph, v_in, v_out, q_all, lab_all, send, got, use, use_t, slot_tab,
    raw_mid, raw_cold, pooled, pooled_t, pre, hidden, resid, vec, vec_t, stat, loss_all, vg,
    q_send, q_part, q_sum, q_recv, pre_g, pool_g, wide, low_t, sg_t, back_send, rs_send,
    rs_got, ph_send, ph_got, ph_acc, fin,
    in_sem, f_s, f_r, q_s, q_r, l_s, l_r, st_s, st_r, qp_s, qp_r, qy_s, qy_r, b_s, b_r,
    w_s, w_r, h_s, h_r, a_s, a_r,
):
    g = lax.axis_index("group")
    r = lax.axis_index("rep")
    me = g * 16 + r
    y, c = g // 2, g % 2
    mate = y * 2 + 1 - c

    def peer(k):
        m = (k * 37) % 128
        pg = ((y + (m // 2) % 4) % 4) * 2 + (c + m % 2) % 2
        pr = ((r // 4 + (m // 8) % 4) % 4) * 4 + (r % 4 + m // 32) % 4
        return pg, pr

    def ship(src, dst, s_sem, r_sem, pg, pr):
        return pltpu.make_async_remote_copy(
            src_ref=src,
            dst_ref=dst,
            send_sem=s_sem,
            recv_sem=r_sem,
            device_id=(pg, pr),
            device_id_type=MESH,
        )

    def loads():
        pairs = (
            (t_hot, v_hot), (p_hot, v_ph), (t_mid, v_mid), (t_cold, v_cold),
            (queries, q_all.at[g]), (w_in, v_in), (w_out, v_out),
        )
        return [pltpu.make_async_copy(a, b, in_sem.at[n]) for n, (a, b) in enumerate(pairs)]

    for copy in loads():
        copy.start()
    barrier = pltpu.get_barrier_semaphore()

    def greet(k, carry):
        pl.semaphore_signal(barrier, inc=1, device_id=peer(k), device_id_type=MESH)
        return carry

    lax.fori_loop(1, 128, greet, 0)
    lab_all[g] = labels[...]
    held = loads()
    for n in range(4):
        held[n].wait()

    lane_seg = lax.broadcasted_iota(jnp.int32, (1, 128), 1) // 32

    def send_rows(k):
        gg = (g + 1 + k) % 8

        def one(j, carry):
            rd = (r + j) % 16
            to = gg * 16 + rd

            @pl.when(to != me)
            def _():
                ship(send.at[to], got.at[me], f_s, f_r, gg, rd).start()

            return carry

        lax.fori_loop(0, 16, one, 0)

    def serve(k, carry):
        gg = (g + 1 + k) % 8
        at = pl.multiple_of(gg * 128, 128)
        idx = cols[pl.ds(at, 128), :]
        hot = mm(picks(idx[:, 0:1], (128, 1024), 1).astype(BF), v_hot[...]).astype(BF)
        rows_hot[pl.ds(at, 128), :] = hot
        near = mm(hot, v_ph[...])
        mid = mm(picks(idx[:, 1:2], (128, 4096), 1).astype(BF), v_mid[...])
        line = mm(picks(idx[:, 2:3] // 4, (128, 4096), 1).astype(BF), v_cold[...])
        line = jnp.where(idx[:, 2:3] % 4 == lane_seg, line, 0.0)
        for n, part in enumerate((near[:, :128], near[:, 128:], mid, line)):
            send[pl.ds(gg * 16, 16), n] = tiled(part).astype(BF)

        @pl.when(k == 1)
        def _():
            pl.semaphore_wait(barrier, 127)

        @pl.when(k > 0)
        def _():
            send_rows(k - 1)

        return carry

    lax.fori_loop(0, 8, serve, 0)
    send_rows(7)
    got[me] = send[me]
    held[4].wait()
    for k in range(1, 4):
        ship(q_all.at[g], q_all.at[g], q_s, q_r.at[0], ((y + k) % 4) * 2 + c, r).start()
    ship(q_all.at[g], q_all.at[g], q_s, q_r.at[1], mate, r).start()
    for k in range(1, 8):
        ship(lab_all.at[g], lab_all.at[g], l_s, l_r, (g + k) % 8, r).start()

    def count_items(i, carry):
        at = pl.multiple_of(i * 128, 128)
        idx = cols[pl.ds(at, 128), :]
        total = picks(idx[:, 4:5], (128, 3072), 1)
        for f in range(5, 8):
            total += picks(idx[:, f : f + 1], (128, 3072), 1)
        use[pl.ds(at, 128), :] = total.astype(BF)
        return carry

    lax.fori_loop(0, 8, count_items, 0)

    def count_slots(i, carry):
        at = pl.multiple_of(i * 256, 256)
        idx = rows[...] - at
        total = picks(idx[0:1], (256, 1024), 0)
        for f in range(1, 4):
            total += picks(idx[f : f + 1], (256, 1024), 0)
        use_t[pl.ds(at, 256), :] = total.astype(BF)
        return carry

    lax.fori_loop(0, 12, count_slots, 0)
    ship(q_all.at[pl.ds(0, 3)], q_all.at[pl.ds(0, 3)], q_s, q_r.at[0], g, r).wait_recv()
    for k in range(1, 4):
        from_y = ((y + k) % 4) * 2 + c
        ship(q_all.at[from_y], q_all.at[from_y], q_s, q_r.at[2], mate, r).start()

    ship(send.at[pl.ds(0, 127)], got.at[pl.ds(0, 127)], f_s, f_r, g, r).wait_recv()

    def fill(i, carry):
        at = pl.multiple_of(i * 256, 256)
        slab = pl.ds(i * 32, 32)
        slot_tab[pl.ds(at, 256), 0:128] = flat(got[slab, 0])
        slot_tab[pl.ds(at, 256), 128:256] = flat(got[slab, 1])
        mid = flat(got[slab, 2])
        raw_mid[pl.ds(at, 256), :] = mid
        slot_tab[pl.ds(1024 + at, 256), :] = mm(mid, p_mid[...]).astype(BF)
        cold = flat(got[slab, 3])
        raw_cold[pl.ds(at, 256), :] = cold
        slot_tab[pl.ds(2048 + at, 256), :] = mm(cold, p_cold[...]).astype(BF)
        return carry

    lax.fori_loop(0, 4, fill, 0)
    held[5].wait()
    held[6].wait()

    def forward(i, carry):
        at = pl.multiple_of(i * 256, 256)
        here = pl.ds(at, 256)
        pool = mm(use[here, :], slot_tab[...])
        low = pool.astype(BF)
        pooled[here, :] = low
        low32 = low.astype(F32)
        pooled_t[:, here] = low32.T.astype(BF)
        u = mm(low, v_in[...])
        pre[here, :] = u
        h = (u * (1.0 / (1.0 + jnp.exp(-u)))).astype(BF)
        hidden[here, :] = h
        res = low32 + mm(h, v_out[...])
        resid[here, :] = res
        inv = lax.rsqrt(jnp.mean(res * res, axis=1, keepdims=True) + NORM_EPS)
        v = res * inv
        vec[here, :] = v.astype(BF)
        vec_t[:, here] = v.T.astype(BF)
        return carry

    lax.fori_loop(0, 4, forward, 0)

    ship(q_all.at[g], q_all.at[g], q_s, q_r.at[1], mate, r).wait_recv()
    ship(q_all.at[pl.ds(0, 3)], q_all.at[pl.ds(0, 3)], q_s, q_r.at[2], g, r).wait_recv()
    ship(lab_all.at[pl.ds(0, 7)], lab_all.at[pl.ds(0, 7)], l_s, l_r, g, r).wait_recv()

    def order(t):
        return (t % 4) * 2 + t // 4

    def send_stat(b):
        for k in range(1, 8):
            ship(stat.at[b, g], stat.at[b, g], st_s, st_r.at[b], (g + k) % 8, r).start()

    def label_rows(b):
        return lab_all[b] - g * 1024

    def stats(t, carry):
        b = order(t)
        st = mm_nt(vec[...], q_all[b])
        top = jnp.max(st, axis=0, keepdims=True)
        total = jnp.sum(jnp.exp2(st * SCALE2 - top * SCALE2), axis=0, keepdims=True)
        hit = label_rows(b) == lax.broadcasted_iota(jnp.int32, st.shape, 0)
        stat[b, g, pl.ds(0, 1), :] = top * LOGIT_SCALE + jnp.log(total)
        picked = jnp.sum(jnp.where(hit, st, 0.0), axis=0, keepdims=True)
        stat[b, g, pl.ds(1, 1), :] = picked * LOGIT_SCALE

        @pl.when(t > 0)
        def _():
            send_stat(order(t - 1))

        return carry

    lax.fori_loop(0, 8, stats, 0)
    send_stat(7)
    vg[...] = jnp.zeros_like(vg)

    def grads(b):
        ship(stat.at[b, pl.ds(0, 7)], stat.at[b, pl.ds(0, 7)], st_s, st_r.at[b], g, r).wait_recv()
        lses = [stat[b, n, pl.ds(0, 1), :] for n in range(8)]
        top = functools.reduce(jnp.maximum, lses)
        total = functools.reduce(jnp.add, [jnp.exp(v - top) for v in lses])
        joint = top + jnp.log(total)
        hits = functools.reduce(jnp.add, [stat[b, n, pl.ds(1, 1), :] for n in range(8)])
        loss_all[b] = joint - hits
        st = mm_nt(vec[...], q_all[b])
        hit = label_rows(b) == lax.broadcasted_iota(jnp.int32, st.shape, 0)
        prob = jnp.exp2((st * LOGIT_SCALE - joint) * 1.4426950408889634)
        grad = (prob - jnp.where(hit, 1.0, 0.0)).astype(BF)
        vg[...] += mm(grad, q_all[b])
        return LOGIT_SCALE * mm(vec_t[...], grad)

    def for_mate(i, carry):
        q_send[i] = grads(((y + 1 + i) % 4) * 2 + 1 - c).astype(BF)
        ship(q_send.at[i], q_part.at[i], qp_s, qp_r.at[i], mate, r).start()
        return carry

    lax.fori_loop(0, 4, for_mate, 0)

    def for_self(i, carry):
        at_y = (y + 1 + i) % 4
        mine = grads(at_y * 2 + c)
        ship(q_send.at[i], q_part.at[i], qp_s, qp_r.at[i], mate, r).wait_recv()
        q_sum[i] = (mine + q_part[i].astype(F32)).astype(BF)

        @pl.when(i < 3)
        def _():
            ship(q_sum.at[i], q_recv.at[i], qy_s, qy_r, at_y * 2 + c, r).start()

        return carry

    lax.fori_loop(0, 4, for_self, 0)
    loss_out[...] = loss_all[g]

    def backward(i, carry):
        at = pl.multiple_of(i * 256, 256)
        here = pl.ds(at, 256)
        res = resid[here, :]
        inv = lax.rsqrt(jnp.mean(res * res, axis=1, keepdims=True) + NORM_EPS)
        grad = LOGIT_SCALE * vg[here, :]
        dot_wide = jnp.sum(grad * res, axis=1, keepdims=True)
        wg = inv * grad - (inv * inv * inv / 256.0) * res * dot_wide
        low = wg.astype(BF)
        low_t[:, here] = wg.T.astype(BF)
        u = pre[here, :]
        s = 1.0 / (1.0 + jnp.exp(-u))
        pg = (mm_nt(low, v_out[...]) * (s * (1.0 + u * (1.0 - s)))).astype(BF)
        pre_g[here, :] = pg
        pool_g[here, :] = (mm_nt(pg, v_in[...]) + wg).astype(BF)
        return carry

    lax.fori_loop(0, 4, backward, 0)

    def send_back(t):
        cc = (t + y) % 4

        def one(j, carry):
            to = cc * 32 + (j + r + 16 * c) % 32

            @pl.when(to != me)
            def _():
                ship(back_send.at[to], back_ref.at[me], b_s, b_r, to // 16, to % 16).start()

            return carry

        lax.fori_loop(0, 32, one, 0)

    def slots(t, carry):
        cc = (t + y) % 4
        at = pl.multiple_of(cc * 256, 256)
        slab = pl.ds(cc * 32, 32)
        hot = mm(use_t[pl.ds(at, 256), :], pool_g[...])
        mid = mm(use_t[pl.ds(1024 + at, 256), :], pool_g[...])
        cold = mm(use_t[pl.ds(2048 + at, 256), :], pool_g[...])
        sg_t[:, pl.ds(at, 256)] = mid.T.astype(BF)
        sg_t[:, pl.ds(1024 + at, 256)] = cold.T.astype(BF)
        b_mid = mm_nt(mid.astype(BF), p_mid[...])
        b_cold = mm_nt(cold.astype(BF), p_cold[...])
        for n, part in enumerate((hot[:, :128], hot[:, 128:], b_mid, b_cold)):
            back_send[slab, n] = tiled(part).astype(BF)

        @pl.when(t > 0)
        def _():
            send_back(t - 1)

        return carry

    lax.fori_loop(0, 4, slots, 0)
    send_back(3)
    back_ref[me] = back_send[me]

    def weights(i, carry):
        at = pl.multiple_of(i * 256, 256)
        first = mm(pooled_t[...], pre_g[:, pl.ds(at, 256)]).T
        for n in range(2):
            part = first[:, 128 * n : 128 * n + 128].reshape(4, 8, 8, 128)
            rs_send[pl.ds(i * 4, 4), :, n] = part.astype(BF)
        second = mm(low_t[...], hidden[:, pl.ds(at, 256)])
        for n in range(2):
            part = second[:, 128 * n : 128 * n + 128].reshape(16, 2, 8, 128).astype(BF)
            rs_send[:, i * 2 + n, 2] = part[:, 0]
            rs_send[:, i * 2 + n, 3] = part[:, 1]
        return carry

    lax.fori_loop(0, 4, weights, 0)
    small = [
        mm(sg_t[:, :1024], raw_mid[...]).reshape(16, 2, 8, 128).astype(BF),
        mm(sg_t[:, 1024:], raw_cold[...]).reshape(16, 2, 8, 128).astype(BF),
    ]
    for n in range(8):
        rs_send[:, n, 4] = small[(n // 2) % 2][:, n % 2]

    def send_blocks(k, carry):
        pg, pr = peer(k)
        ship(rs_send.at[pr, pg], rs_got.at[me], w_s, w_r, pg, pr).start()
        return carry

    lax.fori_loop(1, 128, send_blocks, 0)
    rs_got[me] = rs_send[r, g]
    ship(back_send.at[pl.ds(0, 127)], back_ref.at[pl.ds(0, 127)], b_s, b_r, g, r).wait_recv()
    ph_acc[...] = jnp.zeros_like(ph_acc)

    def hot_weights(i, carry):
        slab = pl.ds(i * 32, 32)
        left = back_ref[slab, 0].astype(F32).reshape(256, 128).T.astype(BF)
        right = back_ref[slab, 1].astype(F32).reshape(256, 128).T.astype(BF)
        own = rows_hot[pl.ds(pl.multiple_of(i * 256, 256), 256), :]
        ph_acc[0:128, :] += mm(left, own)
        ph_acc[128:256, :] += mm(right, own)
        return carry

    lax.fori_loop(0, 4, hot_weights, 0)
    for n in range(4):
        part = ph_acc[:, 128 * n : 128 * n + 128].reshape(16, 2, 8, 128).astype(BF)
        ph_send[:, 2 * n] = part[:, 0]
        ph_send[:, 2 * n + 1] = part[:, 1]

    def send_hot(k, carry):
        pg, pr = peer(k)
        ship(ph_send.at[pr, pg], ph_got.at[me], h_s, h_r, pg, pr).start()
        return carry

    lax.fori_loop(1, 128, send_hot, 0)
    ph_got[me] = ph_send[r, g]

    ship(q_sum.at[pl.ds(0, 3)], q_recv, qy_s, qy_r, g, r).wait_recv()
    qg = q_sum[3].astype(F32)
    for n in range(3):
        qg += q_recv[n].astype(F32)
    qg_out[...] = qg

    ship(rs_got.at[pl.ds(0, 127)], rs_got.at[pl.ds(0, 127)], w_s, w_r, g, r).wait_recv()

    def add(k, total):
        return total + rs_got[k].astype(F32)

    fin[g, pl.ds(0, 5)] = lax.fori_loop(0, 128, add, jnp.zeros((5, 8, 128), F32))
    ship(ph_got.at[pl.ds(0, 127)], ph_got.at[pl.ds(0, 127)], h_s, h_r, g, r).wait_recv()

    def add_hot(k, total):
        return total + ph_got[k].astype(F32)

    fin[g, 5] = lax.fori_loop(0, 128, add_hot, jnp.zeros((8, 128), F32))
    for k in range(1, 8):
        ship(fin.at[g], fin.at[g], a_s, a_r, (g + k) % 8, r).start()
    ship(fin.at[pl.ds(0, 7)], fin.at[pl.ds(0, 7)], a_s, a_r, g, r).wait()
    fin_ref[...] = fin[...]

    ship(send.at[pl.ds(0, 127)], got.at[pl.ds(0, 127)], f_s, f_r, g, r).wait_send()
    ship(q_all.at[pl.ds(0, 7)], q_all.at[pl.ds(0, 7)], q_s, q_r.at[0], g, r).wait_send()
    ship(lab_all.at[pl.ds(0, 7)], lab_all.at[pl.ds(0, 7)], l_s, l_r, g, r).wait_send()
    for b in range(8):
        ship(stat.at[b, pl.ds(0, 7)], stat.at[b, pl.ds(0, 7)], st_s, st_r.at[0], g, r).wait_send()
    ship(q_send, q_part, qp_s, qp_r.at[0], g, r).wait_send()
    ship(q_sum.at[pl.ds(0, 3)], q_recv, qy_s, qy_r, g, r).wait_send()
    ship(back_send.at[pl.ds(0, 127)], back_ref.at[pl.ds(0, 127)], b_s, b_r, g, r).wait_send()
    ship(rs_got.at[pl.ds(0, 127)], rs_got.at[pl.ds(0, 127)], w_s, w_r, g, r).wait_send()
    ship(ph_got.at[pl.ds(0, 127)], ph_got.at[pl.ds(0, 127)], h_s, h_r, g, r).wait_send()


def scatter_kernel(back, served, segs, p_hot, out_hot, out_mid, out_cold, b_hot, b_mid, b_cold):
    step = pl.program_id(0)

    @pl.when(step == 0)
    def _():
        lane_seg = lax.broadcasted_iota(jnp.int32, (1, 128), 1) // 32
        for i in range(4):
            here = pl.ds(i * 256, 256)
            slab = pl.ds(i * 32, 32)
            b_hot[here, :] = (
                mm_nt(flat(back[slab, 0]), p_hot[:, 0:128])
                + mm_nt(flat(back[slab, 1]), p_hot[:, 128:256])
            ).astype(BF)
            b_mid[here, :] = flat(back[slab, 2])
            cold = flat(back[slab, 3])
            b_cold[here, :] = jnp.where(segs[here, 3:4] == lane_seg, cold, jnp.zeros((), BF))

    idx = served[...]
    hot = picks(idx[0:1] - step * 128, (128, 1024), 0).astype(BF)
    out_hot[...] = mm(hot, b_hot[...])
    mid = picks(idx[1:2] - step * 512, (512, 1024), 0).astype(BF)
    out_mid[...] = mm(mid, b_mid[...])
    cold = picks(idx[2:3] - step * 512, (512, 1024), 0).astype(BF)
    out_cold[...] = mm(cold, b_cold[...])


def local(
    table_hot,
    table_mid,
    table_cold,
    proj_hot,
    proj_mid,
    proj_cold,
    tower_in,
    tower_out,
    queries,
    labels,
    item_slot,
    item_block,
    serve_rows,
):
    served = serve_rows[0]
    where = item_block[0] * 1024 + item_slot[0]
    segs = served[2:3] % 4
    cols = jnp.concatenate([served, segs, where], axis=0).T
    idx_rows = jnp.concatenate([served[0:2], served[2:3] // 4, segs], axis=0)
    pc4 = jnp.concatenate([proj_cold] * 4, axis=0)
    anywhere = pl.BlockSpec(memory_space=pl.ANY)
    vmem = pl.BlockSpec(memory_space=pltpu.VMEM)
    sds = jax.ShapeDtypeStruct
    V = pltpu.VMEM
    back, _, qg_t, loss, fin = pl.pallas_call(
        step_kernel,
        out_shape=[
            sds((128, 4, 8, 128), BF),
            sds((1024, 512), BF),
            sds((256, 512), F32),
            sds((1, 512), F32),
            sds((8, 6, 8, 128), F32),
        ],
        in_specs=[anywhere] * 4 + [vmem] * 2 + [anywhere] * 3 + [vmem] * 3,
        out_specs=[vmem] * 5,
        scratch_shapes=[
            V((1024, 512), BF), V((4096, 128), BF), V((4096, 128), BF), V((512, 256), BF),
            V((256, 1024), BF), V((1024, 256), BF), V((8, 512, 256), BF), V((8, 1, 512), jnp.int32),
            V((128, 4, 8, 128), BF), V((128, 4, 8, 128), BF), V((1024, 3072), BF),
            V((3072, 1024), BF), V((3072, 256), BF), V((1024, 128), BF), V((1024, 128), BF),
            V((1024, 256), BF), V((256, 1024), BF), V((1024, 1024), F32), V((1024, 1024), BF),
            V((1024, 256), F32), V((1024, 256), BF), V((256, 1024), BF), V((8, 8, 2, 512), F32),
            V((8, 1, 512), F32), V((1024, 256), F32), V((4, 256, 512), BF), V((4, 256, 512), BF),
            V((4, 256, 512), BF), V((3, 256, 512), BF), V((1024, 1024), BF), V((1024, 256), BF),
            V((8, 128), F32), V((256, 1024), BF), V((256, 2048), BF), V((128, 4, 8, 128), BF),
            V((16, 8, 5, 8, 128), BF), V((128, 5, 8, 128), BF), V((16, 8, 8, 128), BF),
            V((128, 8, 128), BF), V((256, 512), F32), V((8, 6, 8, 128), F32),
            DMA((7,)), DMA, DMA, DMA, DMA((3,)), DMA, DMA, DMA, DMA((8,)), DMA, DMA((4,)),
            DMA, DMA, DMA, DMA, DMA, DMA, DMA, DMA, DMA, DMA,
        ],
        compiler_params=pltpu.CompilerParams(
            collective_id=1, has_side_effects=True, vmem_limit_bytes=63 << 20
        ),
        name="step",
    )(
        table_hot, table_mid, table_cold, proj_hot, proj_mid, pc4, tower_in, tower_out, queries,
        labels.reshape(1, 512), cols, where,
    )
    full = lambda a: pl.BlockSpec(a.shape, lambda i: (0,) * a.ndim)
    grad_hot, grad_mid, grad_cold = pl.pallas_call(
        scatter_kernel,
        grid=(8,),
        in_specs=[full(back), full(idx_rows), full(cols), full(proj_hot)],
        out_specs=[
            pl.BlockSpec((128, 512), lambda i: (i, 0)),
            pl.BlockSpec((512, 128), lambda i: (i, 0)),
            pl.BlockSpec((512, 128), lambda i: (i, 0)),
        ],
        out_shape=[sds((1024, 512), F32), sds((4096, 128), F32), sds((4096, 128), F32)],
        scratch_shapes=[V((1024, 512), BF), V((1024, 128), BF), V((1024, 128), BF)],
        compiler_params=pltpu.CompilerParams(
            dimension_semantics=("arbitrary",), vmem_limit_bytes=40 << 20
        ),
        name="scatter",
    )(back, idx_rows, cols, proj_hot)
    g_in = fin[:, 0:2].transpose(1, 3, 0, 2).reshape(256, 64)
    g_out = fin[:, 2:4].transpose(0, 3, 1, 2).reshape(1024, 16)
    pmc = fin[0:4, 4].reshape(2, 2, 8, 128).transpose(0, 3, 1, 2).reshape(2, 128, 16)
    g_pm = pmc[0]
    g_pc = pmc[1].reshape(4, 32, 16).sum(axis=0)
    g_ph = fin[:, 5].reshape(4, 2, 8, 128).transpose(0, 3, 1, 2).reshape(512, 16)
    return (
        loss[0],
        qg_t.T,
        grad_hot,
        grad_mid,
        grad_cold,
        g_ph,
        g_pm,
        g_pc,
        g_in,
        g_out,
    )


def solution(mesh):
    split = P(BOTH)
    return jax.shard_map(
        local,
        mesh=mesh,
        in_specs=(split,) * 3 + (P(),) * 5 + (split,) * 5,
        out_specs=(split,) * 5 + (P(None, "rep"),) * 5,
        check_vma=False,
    )
```

profile of v0, /device:TPU:1, one launch (start us, length us, event | category | flops | bytes accessed | tf_op | source)
XLA Modules:
  0.0 147.3 jit_solution(14189073572601527970)
XLA Ops:
  0.6 0.7 slice.35
  1.4 0.7 and_select_fusion
  2.1 0.7 add_bitcast_fusion.rows
  2.8 0.0 copy-start.3
  2.8 0.7 copy.64
  3.6 1.5 %pad_maximum_fusion.p_cold = bf16[128,256]{1,0:T(8,128)(2,1)} fusion(bf16[32,256]{1,0:T(8,128)(2,1)} %param.18), kind=kLoop, calls=%fused_computation.1 | loop fusion | flops 262144 | bytes 81920 | tf_op jit(solution)/shard_map/concatenate | solution.py:479
  5.1 1.0 copy.48
  6.1 0.0 copy-done.3
  6.1 0.0 copy-start.1
  6.1 124.4 %step.1 = (bf16[128,4,8,128]{3,2,1,0:T(8,128)(2,1)}, bf16[1024,512]{1,0:T(8,128)(2,1)}, f32[256,512]{1,0:T(8,128)}, f32[1,512]{1,0:T(1,128)}, f32[8,6,8,128]{3,2,1,0:T(8,128)}) custom-call(bf16[1024,512]{1,0:T(8,128)(2,1)} %t_hot.1, bf16[4096,128]{1,0:T(8,128)(2,1)} %t_mid.1, bf16[4096,128]{1,0:T(8,128)(2,1)} %t_cold.1, bf16[512,256]{1,0:T(8,128)(2,1)} %p_hot.3, ...), custom_call_target="tpu_custom_call" | custom-call | tf_op jit(solution)/shard_map/step/pallas_call | solution.py:484
  130.5 0.0 copy-start
  130.5 0.0 copy-start.2
  130.5 0.0 copy-start.4
  130.5 2.2 %copy.52 = f32[512,256]{1,0:T(8,128)} copy(f32[512,256]{0,1:T(8,128)} %bitcast.56) | data formatting | bytes 1048576
  132.6 0.7 slice.38
  133.4 0.6 fusion
  134.0 0.1 reshape_squeeze.11
  134.0 0.6 reduce_sum.9
  134.7 0.8 slice.37
  135.4 1.5 %slice_bitcast_fusion = (f32[8,128,2,8]{1,3,2,0:T(8,128)S(1)}, f32[256,64]{0,1:T(8,128)}) fusion(f32[8,6,8,128]{3,2,1,0:T(8,128)} %get-tuple-element.23), kind=kLoop, calls=%fused_computation.3 | loop fusion | bytes 262144 | tf_op jit(solution)/shard_map/transpose | solution.py:536
  137.0 0.6 copy.61
  137.6 0.6 copy.63
  138.2 0.0 copy-done.1
  138.2 0.0 copy-done
  138.2 0.0 copy-done.2
  138.2 8.4 %scatter.1 = (f32[1024,512]{1,0:T(8,128)}, f32[4096,128]{1,0:T(8,128)}, f32[4096,128]{1,0:T(8,128)}) custom-call(bf16[128,4,8,128]{3,2,1,0:T(8,128)(2,1)S(1)} %copy-done.2, s32[4,1024]{1,0:T(4,128)S(1)} %pad_add_fusion.1.served, s32[1024,8]{1,0:T(8,128)S(1)} %bitcast.55, bf16[512,256]{1,0:T(8,128)(2,1)S(1)} %copy-done.1), custom_call_target="tpu_custom_call" | custom-call | tf_op jit(solution)/shard_map/scatter/pallas_call | solution.py:519
  146.7 0.0 copy-done.4
  146.7 0.6 copy.67
  (5 shorter events, 0.1 us)
Async XLA Ops:
  2.8 3.2 %copy-start.3 = (s32[4,1024]{1,0:T(4,128)}, s32[4,1024]{1,0:T(4,128)S(1)}, u32[]{:S(2)}) copy-start(s32[4,1024]{1,0:T(4,128)S(1)} %add_bitcast_fusion.rows) | copy-start | bytes 49156
  6.1 132.1 %copy-start.1 = (bf16[512,256]{1,0:T(8,128)(2,1)S(1)}, bf16[512,256]{1,0:T(8,128)(2,1)}, u32[]{:S(2)}) copy-start(bf16[512,256]{1,0:T(8,128)(2,1)} %p_hot.3) | copy-start | bytes 786436
  130.5 7.8 %copy-start = (s32[8,1024]{0,1:T(8,128)S(1)}, s32[8,1024]{0,1:T(8,128)}, u32[]{:S(2)}) copy-start(s32[8,1024]{0,1:T(8,128)} %copy.48) | copy-start | bytes 98308
  130.5 7.8 %copy-start.2 = (bf16[128,4,8,128]{3,2,1,0:T(8,128)(2,1)S(1)}, bf16[128,4,8,128]{3,2,1,0:T(8,128)(2,1)}, u32[]{:S(2)}) copy-start(bf16[128,4,8,128]{3,2,1,0:T(8,128)(2,1)} %get-tuple-element.19.back) | copy-start | bytes 3145732
  130.5 16.2 %copy-start.4 = (f32[1,512]{1,0:T(1,128)S(1)}, f32[1,512]{1,0:T(1,128)}, u32[]{:S(2)}) copy-start(f32[1,512]{1,0:T(1,128)} %get-tuple-element.17) | copy-start | bytes 6148
where the time goes:
time: 148 us; the launch traced here: 147 us
  Pallas kernels  133 us (90%)
  local copies, waits for them, and re-layouts  10.1 us (7%)
  other arithmetic  3.62 us (2%)
    pallas_call x1, Pallas kernels, local(): pl.pallas_call(step_kernel, out_shape=[sds((128, 4, 8, 128), BF), sds((10...  124 us
    pallas_call x1, Pallas kernels, local(): pl.pallas_call(scatter_kernel, grid=(8,), in_specs=[full(back), full(idx_...  8.44 us
    unnamed x15, local copies, waits for them, and re-layouts  4.12 us

commit v1 on v0

--- a/solution.py
+++ b/solution.py
@@ -39,19 +39,24 @@
     return value.reshape(value.shape[0] // 8, 8, value.shape[1])
 
 
+def to_col(row):
+    return jnp.broadcast_to(row.astype(F32), (128, row.shape[1])).T[:, 0:1].astype(jnp.int32)
+
+
 def picks(index, shape, axis):
     return jnp.where(index == lax.broadcasted_iota(jnp.int32, shape, axis), 1.0, 0.0)
 
 
 def step_kernel(
-    t_hot, t_mid, t_cold, p_hot, p_mid, p_cold, w_in, w_out, queries, labels, cols, rows,
+    t_hot, t_mid, t_cold, p_hot, p_mid, proj_cold, w_in, w_out, queries, labels, served,
+    item_slot, item_block,
     back_ref, rows_hot, qg_out, loss_out, fin_ref,
-    v_hot, v_mid, v_cold, v_ph, v_in, v_out, q_all, lab_all, send, got, use, use_t, slot_tab,
-    raw_mid, raw_cold, pooled, pooled_t, pre, hidden, resid, vec, vec_t, stat, loss_all, vg,
-    q_send, q_part, q_sum, q_recv, pre_g, pool_g, wide, low_t, sg_t, back_send, rs_send,
-    rs_got, ph_send, ph_got, ph_acc, fin,
+    v_hot, v_mid, v_cold, v_ph, v_in, v_out, q_all, lab_all, send, got, use_t, slot_t,
+    raw_mid, raw_cold, p_cold, p_mid_t, p_cold_t, pooled_t, pre, hidden, resid, vec, vec_t, stat, loss_all, vg,
+    q_send, q_part, q_sum, q_recv, pre_g, pool_g, low_t, sg_t, back_send, rs_part,
+    rs_pair, rs_send, rs_got, ph_send, ph_got, ph_acc, fin,
     in_sem, f_s, f_r, q_s, q_r, l_s, l_r, st_s, st_r, qp_s, qp_r, qy_s, qy_r, b_s, b_r,
-    w_s, w_r, h_s, h_r, a_s, a_r,
+    wp_s, wp_r, w_s, w_r, h_s, h_r, a_s, a_r,
 ):
     g = lax.axis_index("group")
     r = lax.axis_index("rep")
@@ -59,11 +64,15 @@
     y, c = g // 2, g % 2
     mate = y * 2 + 1 - c
 
-    def peer(k):
-        m = (k * 37) % 128
-        pg = ((y + (m // 2) % 4) % 4) * 2 + (c + m % 2) % 2
-        pr = ((r // 4 + (m // 8) % 4) % 4) * 4 + (r % 4 + m // 32) % 4
-        return pg, pr
+    def all_peers(visit, step=1):
+        for k in range(0, 8, step):
+            pg = lax.rem(g + k, 8)
+
+            def one(j, carry, pg=pg):
+                visit(pg, lax.rem(r + j, 16))
+                return carry
+
+            lax.fori_loop(0 if k else 1, 16, one, 0)
 
     def ship(src, dst, s_sem, r_sem, pg, pr):
         return pltpu.make_async_remote_copy(
@@ -77,7 +86,11 @@
 
     def loads():
         pairs = (
-            (t_hot, v_hot), (p_hot, v_ph), (t_mid, v_mid), (t_cold, v_cold),
+            (t_hot, v_hot), (p_hot, v_ph),
+            (t_mid.at[pl.ds(0, 2048)], v_mid.at[:, pl.ds(0, 128)]),
+            (t_mid.at[pl.ds(2048, 2048)], v_mid.at[:, pl.ds(128, 128)]),
+            (t_cold.at[pl.ds(0, 2048)], v_cold.at[:, pl.ds(0, 128)]),
+            (t_cold.at[pl.ds(2048, 2048)], v_cold.at[:, pl.ds(128, 128)]),
             (queries, q_all.at[g]), (w_in, v_in), (w_out, v_out),
         )
         return [pltpu.make_async_copy(a, b, in_sem.at[n]) for n, (a, b) in enumerate(pairs)]
@@ -86,14 +99,17 @@
         copy.start()
     barrier = pltpu.get_barrier_semaphore()
 
-    def greet(k, carry):
-        pl.semaphore_signal(barrier, inc=1, device_id=peer(k), device_id_type=MESH)
-        return carry
-
-    lax.fori_loop(1, 128, greet, 0)
+    def greet(pg, pr):
+        pl.semaphore_signal(barrier, inc=1, device_id=(pg, pr), device_id_type=MESH)
+
+    all_peers(greet)
     lab_all[g] = labels[...]
     held = loads()
     for n in range(4):
+        p_cold[pl.ds(32 * n, 32), :] = proj_cold[...]
+    p_mid_t[...] = p_mid[...].astype(F32).T.astype(BF)
+    p_cold_t[...] = p_cold[...].astype(F32).T.astype(BF)
+    for n in range(6):
         held[n].wait()
 
     lane_seg = lax.broadcasted_iota(jnp.int32, (1, 128), 1) // 32
@@ -113,53 +129,42 @@
 
         lax.fori_loop(0, 16, one, 0)
 
+    def halves(index, table):
+        both = mm(picks(index % 2048, (128, 2048), 1).astype(BF), table[...])
+        return jnp.where(index >= 2048, both[:, 128:], both[:, :128])
+
     def serve(k, carry):
         gg = (g + 1 + k) % 8
         at = pl.multiple_of(gg * 128, 128)
-        idx = cols[pl.ds(at, 128), :]
-        hot = mm(picks(idx[:, 0:1], (128, 1024), 1).astype(BF), v_hot[...]).astype(BF)
-        rows_hot[pl.ds(at, 128), :] = hot
+        here = pl.ds(at, 128)
+        i_hot, i_mid, i_cold = [to_col(served[pl.ds(n, 1), here]) for n in range(3)]
+        hot = mm(picks(i_hot, (128, 1024), 1).astype(BF), v_hot[...]).astype(BF)
+        rows_hot[here, :] = hot
         near = mm(hot, v_ph[...])
-        mid = mm(picks(idx[:, 1:2], (128, 4096), 1).astype(BF), v_mid[...])
-        line = mm(picks(idx[:, 2:3] // 4, (128, 4096), 1).astype(BF), v_cold[...])
-        line = jnp.where(idx[:, 2:3] % 4 == lane_seg, line, 0.0)
+        mid = halves(i_mid, v_mid)
+        line = halves(i_cold // 4, v_cold)
+        line = jnp.where(i_cold % 4 == lane_seg, line, 0.0)
         for n, part in enumerate((near[:, :128], near[:, 128:], mid, line)):
             send[pl.ds(gg * 16, 16), n] = tiled(part).astype(BF)
-
-        @pl.when(k == 1)
-        def _():
-            pl.semaphore_wait(barrier, 127)
-
-        @pl.when(k > 0)
-        def _():
-            send_rows(k - 1)
-
         return carry
 
     lax.fori_loop(0, 8, serve, 0)
-    send_rows(7)
+    pl.semaphore_wait(barrier, 127)
+    for k in range(8):
+        send_rows(k)
     got[me] = send[me]
-    held[4].wait()
+    held[6].wait()
     for k in range(1, 4):
         ship(q_all.at[g], q_all.at[g], q_s, q_r.at[0], ((y + k) % 4) * 2 + c, r).start()
     ship(q_all.at[g], q_all.at[g], q_s, q_r.at[1], mate, r).start()
     for k in range(1, 8):
         ship(lab_all.at[g], lab_all.at[g], l_s, l_r, (g + k) % 8, r).start()
 
-    def count_items(i, carry):
-        at = pl.multiple_of(i * 128, 128)
-        idx = cols[pl.ds(at, 128), :]
-        total = picks(idx[:, 4:5], (128, 3072), 1)
-        for f in range(5, 8):
-            total += picks(idx[:, f : f + 1], (128, 3072), 1)
-        use[pl.ds(at, 128), :] = total.astype(BF)
-        return carry
-
-    lax.fori_loop(0, 8, count_items, 0)
+    where = item_block[...] * 1024 + item_slot[...]
 
     def count_slots(i, carry):
         at = pl.multiple_of(i * 256, 256)
-        idx = rows[...] - at
+        idx = where - at
         total = picks(idx[0:1], (256, 1024), 0)
         for f in range(1, 4):
             total += picks(idx[f : f + 1], (256, 1024), 0)
@@ -177,28 +182,28 @@
     def fill(i, carry):
         at = pl.multiple_of(i * 256, 256)
         slab = pl.ds(i * 32, 32)
-        slot_tab[pl.ds(at, 256), 0:128] = flat(got[slab, 0])
-        slot_tab[pl.ds(at, 256), 128:256] = flat(got[slab, 1])
+        for n in range(2):
+            near = got[slab, n].astype(F32).reshape(256, 128).T.astype(BF)
+            slot_t[pl.ds(128 * n, 128), pl.ds(at, 256)] = near
         mid = flat(got[slab, 2])
         raw_mid[pl.ds(at, 256), :] = mid
-        slot_tab[pl.ds(1024 + at, 256), :] = mm(mid, p_mid[...]).astype(BF)
+        slot_t[:, pl.ds(1024 + at, 256)] = mm_nt(p_mid_t[...], mid).astype(BF)
         cold = flat(got[slab, 3])
         raw_cold[pl.ds(at, 256), :] = cold
-        slot_tab[pl.ds(2048 + at, 256), :] = mm(cold, p_cold[...]).astype(BF)
+        slot_t[:, pl.ds(2048 + at, 256)] = mm_nt(p_cold_t[...], cold).astype(BF)
         return carry
 
     lax.fori_loop(0, 4, fill, 0)
-    held[5].wait()
-    held[6].wait()
+    held[7].wait()
+    held[8].wait()
 
     def forward(i, carry):
         at = pl.multiple_of(i * 256, 256)
         here = pl.ds(at, 256)
-        pool = mm(use[here, :], slot_tab[...])
-        low = pool.astype(BF)
-        pooled[here, :] = low
-        low32 = low.astype(F32)
-        pooled_t[:, here] = low32.T.astype(BF)
+        turned = mm(slot_t[...], use_t[:, here]).astype(BF)
+        pooled_t[:, here] = turned
+        low32 = turned.astype(F32).T
+        low = low32.astype(BF)
         u = mm(low, v_in[...])
         pre[here, :] = u
         h = (u * (1.0 / (1.0 + jnp.exp(-u)))).astype(BF)
@@ -345,13 +350,14 @@
         at = pl.multiple_of(i * 256, 256)
         first = mm(pooled_t[...], pre_g[:, pl.ds(at, 256)]).T
         for n in range(2):
-            part = first[:, 128 * n : 128 * n + 128].reshape(4, 8, 8, 128)
-            rs_send[pl.ds(i * 4, 4), :, n] = part.astype(BF)
+            part = first[:, 128 * n : 128 * n + 128].reshape(4, 4, 2, 8, 128).astype(BF)
+            for e in range(2):
+                rs_part[e, pl.ds(i * 4, 4), :, n] = part[:, :, e]
         second = mm(low_t[...], hidden[:, pl.ds(at, 256)])
-        for n in range(2):
-            part = second[:, 128 * n : 128 * n + 128].reshape(16, 2, 8, 128).astype(BF)
-            rs_send[:, i * 2 + n, 2] = part[:, 0]
-            rs_send[:, i * 2 + n, 3] = part[:, 1]
+        for e in range(2):
+            part = second[:, 128 * e : 128 * e + 128].reshape(16, 2, 8, 128).astype(BF)
+            rs_part[e, :, i, 2] = part[:, 0]
+            rs_part[e, :, i, 3] = part[:, 1]
         return carry
 
     lax.fori_loop(0, 4, weights, 0)
@@ -360,15 +366,22 @@
         mm(sg_t[:, 1024:], raw_cold[...]).reshape(16, 2, 8, 128).astype(BF),
     ]
     for n in range(8):
-        rs_send[:, n, 4] = small[(n // 2) % 2][:, n % 2]
-
-    def send_blocks(k, carry):
-        pg, pr = peer(k)
-        ship(rs_send.at[pr, pg], rs_got.at[me], w_s, w_r, pg, pr).start()
-        return carry
-
-    lax.fori_loop(1, 128, send_blocks, 0)
-    rs_got[me] = rs_send[r, g]
+        rs_part[n % 2, :, n // 2, 4] = small[(n // 2) % 2][:, n % 2]
+    ship(rs_part.at[1 - c], rs_pair, wp_s, wp_r, mate, r).start()
+    ship(rs_part.at[1 - c], rs_pair, wp_s, wp_r, mate, r).wait()
+
+    def add_pair(k, carry):
+        rs_send[k] = (rs_part[c, k].astype(F32) + rs_pair[k].astype(F32)).astype(BF)
+        return carry
+
+    lax.fori_loop(0, 16, add_pair, 0)
+    src = r * 4 + y
+
+    def send_block(pg, pr):
+        ship(rs_send.at[pr, pg // 2], rs_got.at[src], w_s, w_r, pg, pr).start()
+
+    all_peers(send_block, 2)
+    rs_got[src] = rs_send[r, y]
     ship(back_send.at[pl.ds(0, 127)], back_ref.at[pl.ds(0, 127)], b_s, b_r, g, r).wait_recv()
     ph_acc[...] = jnp.zeros_like(ph_acc)
 
@@ -387,12 +400,10 @@
         ph_send[:, 2 * n] = part[:, 0]
         ph_send[:, 2 * n + 1] = part[:, 1]
 
-    def send_hot(k, carry):
-        pg, pr = peer(k)
+    def send_hot(pg, pr):
         ship(ph_send.at[pr, pg], ph_got.at[me], h_s, h_r, pg, pr).start()
-        return carry
-
-    lax.fori_loop(1, 128, send_hot, 0)
+
+    all_peers(send_hot)
     ph_got[me] = ph_send[r, g]
 
     ship(q_sum.at[pl.ds(0, 3)], q_recv, qy_s, qy_r, g, r).wait_recv()
@@ -401,12 +412,12 @@
         qg += q_recv[n].astype(F32)
     qg_out[...] = qg
 
-    ship(rs_got.at[pl.ds(0, 127)], rs_got.at[pl.ds(0, 127)], w_s, w_r, g, r).wait_recv()
+    ship(rs_got.at[pl.ds(0, 63)], rs_got.at[pl.ds(0, 63)], w_s, w_r, g, r).wait_recv()
 
     def add(k, total):
         return total + rs_got[k].astype(F32)
 
-    fin[g, pl.ds(0, 5)] = lax.fori_loop(0, 128, add, jnp.zeros((5, 8, 128), F32))
+    fin[g, pl.ds(0, 5)] = lax.fori_loop(0, 64, add, jnp.zeros((5, 8, 128), F32))
     ship(ph_got.at[pl.ds(0, 127)], ph_got.at[pl.ds(0, 127)], h_s, h_r, g, r).wait_recv()
 
     def add_hot(k, total):
@@ -426,34 +437,59 @@
     ship(q_send, q_part, qp_s, qp_r.at[0], g, r).wait_send()
     ship(q_sum.at[pl.ds(0, 3)], q_recv, qy_s, qy_r, g, r).wait_send()
     ship(back_send.at[pl.ds(0, 127)], back_ref.at[pl.ds(0, 127)], b_s, b_r, g, r).wait_send()
-    ship(rs_got.at[pl.ds(0, 127)], rs_got.at[pl.ds(0, 127)], w_s, w_r, g, r).wait_send()
+    ship(rs_got.at[pl.ds(0, 63)], rs_got.at[pl.ds(0, 63)], w_s, w_r, g, r).wait_send()
     ship(ph_got.at[pl.ds(0, 127)], ph_got.at[pl.ds(0, 127)], h_s, h_r, g, r).wait_send()
 
 
-def scatter_kernel(back, served, segs, p_hot, out_hot, out_mid, out_cold, b_hot, b_mid, b_cold):
+def scatter_kernel(
+    back, served, p_hot, fin, qg_t, loss,
+    out_hot, out_mid, out_cold, out_qg, out_loss, o_ph, o_pm, o_pc, o_in, o_out,
+    b_hot, b_mid, b_cold,
+):
     step = pl.program_id(0)
 
     @pl.when(step == 0)
     def _():
         lane_seg = lax.broadcasted_iota(jnp.int32, (1, 128), 1) // 32
-        for i in range(4):
-            here = pl.ds(i * 256, 256)
-            slab = pl.ds(i * 32, 32)
+        zero = jnp.zeros((), BF)
+        for i in range(8):
+            here = pl.ds(i * 128, 128)
+            slab = pl.ds(i * 16, 16)
             b_hot[here, :] = (
                 mm_nt(flat(back[slab, 0]), p_hot[:, 0:128])
                 + mm_nt(flat(back[slab, 1]), p_hot[:, 128:256])
             ).astype(BF)
-            b_mid[here, :] = flat(back[slab, 2])
-            cold = flat(back[slab, 3])
-            b_cold[here, :] = jnp.where(segs[here, 3:4] == lane_seg, cold, jnp.zeros((), BF))
-
+            i_mid = to_col(served[1:2, here])
+            i_cold = to_col(served[2:3, here])
+            mid = flat(back[slab, 2])
+            cold = jnp.where(i_cold % 4 == lane_seg, flat(back[slab, 3]), zero)
+            for n in range(2):
+                lanes = slice(128 * n, 128 * n + 128)
+                b_mid[here, lanes] = jnp.where(i_mid // 2048 == n, mid, zero)
+                b_cold[here, lanes] = jnp.where(i_cold // 8192 == n, cold, zero)
+        out_loss[...] = loss[...]
+        for n in range(2):
+            o_in[128 * n : 128 * n + 128, :] = fin[:, n].reshape(64, 128).T
+        for n in range(8):
+            o_out[128 * n : 128 * n + 128, :] = fin[n, 2:4].reshape(16, 128).T
+        for n in range(4):
+            o_ph[128 * n : 128 * n + 128, :] = fin[2 * n : 2 * n + 2, 5].reshape(16, 128).T
+        o_pm[...] = fin[0:2, 4].reshape(16, 128).T
+        cold_t = fin[2:4, 4].reshape(16, 128).T
+        o_pc[...] = cold_t[0:32] + cold_t[32:64] + cold_t[64:96] + cold_t[96:128]
+
+    out_qg[...] = qg_t[...].T
     idx = served[...]
-    hot = picks(idx[0:1] - step * 128, (128, 1024), 0).astype(BF)
+    hot = picks(idx[0:1] - step * 256, (256, 1024), 0).astype(BF)
     out_hot[...] = mm(hot, b_hot[...])
-    mid = picks(idx[1:2] - step * 512, (512, 1024), 0).astype(BF)
-    out_mid[...] = mm(mid, b_mid[...])
-    cold = picks(idx[2:3] - step * 512, (512, 1024), 0).astype(BF)
-    out_cold[...] = mm(cold, b_cold[...])
+    mid = picks(idx[1:2] % 2048 - step * 512, (512, 1024), 0).astype(BF)
+    both = mm(mid, b_mid[...])
+    out_mid[0] = both[:, :128]
+    out_mid[1] = both[:, 128:]
+    cold = picks((idx[2:3] // 4) % 2048 - step * 512, (512, 1024), 0).astype(BF)
+    both = mm(cold, b_cold[...])
+    out_cold[0] = both[:, :128]
+    out_cold[1] = both[:, 128:]
 
 
 def local(
@@ -472,11 +508,6 @@
     serve_rows,
 ):
     served = serve_rows[0]
-    where = item_block[0] * 1024 + item_slot[0]
-    segs = served[2:3] % 4
-    cols = jnp.concatenate([served, segs, where], axis=0).T
-    idx_rows = jnp.concatenate([served[0:2], served[2:3] // 4, segs], axis=0)
-    pc4 = jnp.concatenate([proj_cold] * 4, axis=0)
     anywhere = pl.BlockSpec(memory_space=pl.ANY)
     vmem = pl.BlockSpec(memory_space=pltpu.VMEM)
     sds = jax.ShapeDtypeStruct
@@ -490,65 +521,67 @@
             sds((1, 512), F32),
             sds((8, 6, 8, 128), F32),
         ],
-        in_specs=[anywhere] * 4 + [vmem] * 2 + [anywhere] * 3 + [vmem] * 3,
+        in_specs=[anywhere] * 4 + [vmem] * 2 + [anywhere] * 3 + [vmem] * 4,
         out_specs=[vmem] * 5,
         scratch_shapes=[
-            V((1024, 512), BF), V((4096, 128), BF), V((4096, 128), BF), V((512, 256), BF),
+            V((1024, 512), BF), V((2048, 256), BF), V((2048, 256), BF), V((512, 256), BF),
             V((256, 1024), BF), V((1024, 256), BF), V((8, 512, 256), BF), V((8, 1, 512), jnp.int32),
-            V((128, 4, 8, 128), BF), V((128, 4, 8, 128), BF), V((1024, 3072), BF),
-            V((3072, 1024), BF), V((3072, 256), BF), V((1024, 128), BF), V((1024, 128), BF),
-            V((1024, 256), BF), V((256, 1024), BF), V((1024, 1024), F32), V((1024, 1024), BF),
-            V((1024, 256), F32), V((1024, 256), BF), V((256, 1024), BF), V((8, 8, 2, 512), F32),
-            V((8, 1, 512), F32), V((1024, 256), F32), V((4, 256, 512), BF), V((4, 256, 512), BF),
-            V((4, 256, 512), BF), V((3, 256, 512), BF), V((1024, 1024), BF), V((1024, 256), BF),
-            V((8, 128), F32), V((256, 1024), BF), V((256, 2048), BF), V((128, 4, 8, 128), BF),
-            V((16, 8, 5, 8, 128), BF), V((128, 5, 8, 128), BF), V((16, 8, 8, 128), BF),
-            V((128, 8, 128), BF), V((256, 512), F32), V((8, 6, 8, 128), F32),
-            DMA((7,)), DMA, DMA, DMA, DMA((3,)), DMA, DMA, DMA, DMA((8,)), DMA, DMA((4,)),
-            DMA, DMA, DMA, DMA, DMA, DMA, DMA, DMA, DMA, DMA,
+            V((128, 4, 8, 128), BF), V((128, 4, 8, 128), BF), V((3072, 1024), BF),
+            V((256, 3072), BF), V((1024, 128), BF), V((1024, 128), BF), V((128, 256), BF),
+            V((256, 128), BF), V((256, 128), BF), V((256, 1024), BF), V((1024, 1024), F32),
+            V((1024, 1024), BF), V((1024, 256), F32), V((1024, 256), BF), V((256, 1024), BF),
+            V((8, 8, 2, 512), F32), V((8, 1, 512), F32), V((1024, 256), F32),
+            V((4, 256, 512), BF), V((4, 256, 512), BF), V((4, 256, 512), BF),
+            V((3, 256, 512), BF), V((1024, 1024), BF), V((1024, 256), BF), V((256, 1024), BF),
+            V((256, 2048), BF), V((128, 4, 8, 128), BF), V((2, 16, 4, 5, 8, 128), BF),
+            V((16, 4, 5, 8, 128), BF), V((16, 4, 5, 8, 128), BF), V((64, 5, 8, 128), BF),
+            V((16, 8, 8, 128), BF), V((128, 8, 128), BF), V((256, 512), F32),
+            V((8, 6, 8, 128), F32),
+            DMA((9,)), DMA, DMA, DMA, DMA((3,)), DMA, DMA, DMA, DMA((8,)), DMA, DMA((4,)),
+            DMA, DMA, DMA, DMA, DMA, DMA, DMA, DMA, DMA, DMA, DMA, DMA,
         ],
         compiler_params=pltpu.CompilerParams(
             collective_id=1, has_side_effects=True, vmem_limit_bytes=63 << 20
         ),
         name="step",
     )(
-        table_hot, table_mid, table_cold, proj_hot, proj_mid, pc4, tower_in, tower_out, queries,
-        labels.reshape(1, 512), cols, where,
+        table_hot, table_mid, table_cold, proj_hot, proj_mid, proj_cold, tower_in, tower_out,
+        queries, labels.reshape(1, 512), served, item_slot[0], item_block[0],
     )
     full = lambda a: pl.BlockSpec(a.shape, lambda i: (0,) * a.ndim)
-    grad_hot, grad_mid, grad_cold = pl.pallas_call(
+    outs = [
+        sds((1024, 512), F32), sds((2, 2048, 128), F32), sds((2, 2048, 128), F32),
+        sds((512, 256), F32), sds((1, 512), F32), sds((512, 16), F32), sds((128, 16), F32),
+        sds((32, 16), F32), sds((256, 64), F32), sds((1024, 16), F32),
+    ]
+    grad_hot, grad_mid, grad_cold, query_grad, query_loss, *rest = pl.pallas_call(
         scatter_kernel,
-        grid=(8,),
-        in_specs=[full(back), full(idx_rows), full(cols), full(proj_hot)],
+        grid=(4,),
+        in_specs=[
+            full(back), full(served), full(proj_hot), full(fin),
+            pl.BlockSpec((256, 128), lambda i: (0, i)), full(loss),
+        ],
         out_specs=[
-            pl.BlockSpec((128, 512), lambda i: (i, 0)),
-            pl.BlockSpec((512, 128), lambda i: (i, 0)),
-            pl.BlockSpec((512, 128), lambda i: (i, 0)),
-        ],
-        out_shape=[sds((1024, 512), F32), sds((4096, 128), F32), sds((4096, 128), F32)],
-        scratch_shapes=[V((1024, 512), BF), V((1024, 128), BF), V((1024, 128), BF)],
+            pl.BlockSpec((256, 512), lambda i: (i, 0)),
+            pl.BlockSpec((2, 512, 128), lambda i: (0, i, 0)),
+            pl.BlockSpec((2, 512, 128), lambda i: (0, i, 0)),
+            pl.BlockSpec((128, 256), lambda i: (i, 0)),
+        ]
+        + [full(o) for o in outs[4:]],
+        out_shape=outs,
+        scratch_shapes=[V((1024, 512), BF), V((1024, 256), BF), V((1024, 256), BF)],
         compiler_params=pltpu.CompilerParams(
             dimension_semantics=("arbitrary",), vmem_limit_bytes=40 << 20
         ),
         name="scatter",
-    )(back, idx_rows, cols, proj_hot)
-    g_in = fin[:, 0:2].transpose(1, 3, 0, 2).reshape(256, 64)
-    g_out = fin[:, 2:4].transpose(0, 3, 1, 2).reshape(1024, 16)
-    pmc = fin[0:4, 4].reshape(2, 2, 8, 128).transpose(0, 3, 1, 2).reshape(2, 128, 16)
-    g_pm = pmc[0]
-    g_pc = pmc[1].reshape(4, 32, 16).sum(axis=0)
-    g_ph = fin[:, 5].reshape(4, 2, 8, 128).transpose(0, 3, 1, 2).reshape(512, 16)
+    )(back, served, proj_hot, fin, qg_t, loss)
     return (
-        loss[0],
-        qg_t.T,
+        query_loss[0],
+        query_grad,
         grad_hot,
-        grad_mid,
-        grad_cold,
-        g_ph,
-        g_pm,
-        g_pc,
-        g_in,
-        g_out,
+        grad_mid.reshape(4096, 128),
+        grad_cold.reshape(4096, 128),
+        *rest,
     )
 
 

time: 148 us -> 130 us (0.88)
  Pallas kernels: 133 us -> 120 us
  other arithmetic: 3.62 us -> 0 us
    pallas_call x1, Pallas kernels: 124 us -> 113 us  [local(): pl.pallas_call(step_kernel, out_shape=[sds((128, 4, 8, 128), BF), sds((10...]
    unnamed x15 -> x18, local copies, waits for them, and re-layouts: 4.12 us -> 8.71 us
    slice x4 -> x0, local copies, waits for them, and re-layouts: 2.78 us -> none  [the longest x1 0.76 us: local(): fin[:, 5].reshape(4, 2, 8, 128).transpose(0, 3, 1, 2).reshape(512, 16)]
    transpose x3 -> x0, local copies, waits for them, and re-layouts: 2.15 us -> none  [the longest x2 1.53 us: local(): g_out = fin[:, 2:4].transpose(0, 3, 1, 2).reshape(1024, 16)]
    concatenate x3 -> x0, other arithmetic: 1.53 us -> none  [the longest x1 1.5 us: local(): pc4 = jnp.concatenate([proj_cold] * 4, axis=0)]
where the time goes in v1:
time: 130 us; the launch traced here: 129 us
  Pallas kernels  120 us (92%)
  local copies, waits for them, and re-layouts  8.71 us (7%)
    pallas_call x1, Pallas kernels, local(): pl.pallas_call(step_kernel, out_shape=[sds((128, 4, 8, 128), BF), sds((10...  113 us
    unnamed x18, local copies, waits for them, and re-layouts  8.71 us
    pallas_call x1, Pallas kernels, local(): pl.pallas_call(scatter_kernel, grid=(4,), in_specs=[full(back), full(serv...  7.07 us

profile of v1, /device:TPU:1, one launch (start us, length us, event | category | flops | bytes accessed | tf_op | source)
XLA Modules:
  0.0 129.3 jit_solution(15667369712170310242)
XLA Ops:
  0.6 1.3 %copy.30 = s32[1,3,1024]{2,1,0:T(4,128)} copy(s32[1,3,1024]{2,0,1:T(1,128)} %param.25) | data formatting | bytes 24576
  2.0 0.0 copy-start
  2.0 0.0 copy-start.4
  2.0 112.8 %step.1 = (bf16[128,4,8,128]{3,2,1,0:T(8,128)(2,1)}, bf16[1024,512]{1,0:T(8,128)(2,1)}, f32[256,512]{1,0:T(8,128)}, f32[1,512]{1,0:T(1,128)}, f32[8,6,8,128]{3,2,1,0:T(8,128)}) custom-call(bf16[1024,512]{1,0:T(8,128)(2,1)} %t_hot.1, bf16[4096,128]{1,0:T(8,128)(2,1)} %t_mid.1, bf16[4096,128]{1,0:T(8,128)(2,1)} %t_cold.1, bf16[512,256]{1,0:T(8,128)(2,1)} %p_hot.3, ...), custom_call_target="tpu_custom_call" | custom-call | tf_op jit(solution)/shard_map/step/pallas_call | solution.py:515
  114.8 0.0 copy-done
  114.8 0.0 copy-done.4
  114.8 0.0 copy-start.1
  114.8 1.2 copy-done.1
  116.0 0.0 copy-start.2
  116.0 1.0 copy-done.2
  117.1 0.0 copy-start.3
  117.1 0.9 copy-done.3
  118.0 0.0 copy-start.5
  118.0 0.6 copy-done.5
  118.6 7.1 %scatter.1 = (f32[1024,512]{1,0:T(8,128)}, f32[2,2048,128]{2,1,0:T(8,128)}, f32[2,2048,128]{2,1,0:T(8,128)}, f32[512,256]{1,0:T(8,128)}, f32[1,512]{1,0:T(1,128)...) custom-call(bf16[128,4,8,128]{3,2,1,0:T(8,128)(2,1)S(1)} %copy-done., ...), custom_call_target="tpu_custom_call" | custom-call | tf_op jit(solution)/shard_map/scatter/pallas_call | solution.py:557
  125.7 0.7 copy.24
  126.4 0.7 copy.25
  127.1 0.7 copy.23
  127.8 0.7 copy.26
  128.5 0.8 copy.27
Async XLA Ops:
  2.0 112.8 %copy-start = (bf16[512,256]{1,0:T(8,128)(2,1)S(1)}, bf16[512,256]{1,0:T(8,128)(2,1)}, u32[]{:S(2)}) copy-start(bf16[512,256]{1,0:T(8,128)(2,1)} %p_hot.3) | copy-start | bytes 786436
  2.0 112.8 %copy-start.4 = (s32[1,3,1024]{2,1,0:T(4,128)S(1)}, s32[1,3,1024]{2,1,0:T(4,128)}, u32[]{:S(2)}) copy-start(s32[1,3,1024]{2,1,0:T(4,128)} %copy.30) | copy-start | bytes 36868
  114.8 1.2 copy-start.1
  116.0 1.0 copy-start.2
  117.1 0.9 copy-start.3
  118.0 0.6 copy-start.5

commit v2 on v1

--- a/solution.py
+++ b/solution.py
@@ -50,13 +50,14 @@
 def step_kernel(
     t_hot, t_mid, t_cold, p_hot, p_mid, proj_cold, w_in, w_out, queries, labels, served,
     item_slot, item_block,
-    back_ref, rows_hot, qg_out, loss_out, fin_ref,
-    v_hot, v_mid, v_cold, v_ph, v_in, v_out, q_all, lab_all, send, got, use_t, slot_t,
+    back_ref, qg_out, loss_out, fin_ref,
+    v_hot, v_mid, v_cold, v_ph, v_in, v_out, q_all, lab_all, send, got, rows_hot,
+    raw_hot, use_t, slot_t,
     raw_mid, raw_cold, p_cold, p_mid_t, p_cold_t, pooled_t, pre, hidden, resid, vec, vec_t, stat, loss_all, vg,
     q_send, q_part, q_sum, q_recv, pre_g, pool_g, low_t, sg_t, back_send, rs_part,
-    rs_pair, rs_send, rs_got, ph_send, ph_got, ph_acc, fin,
+    rs_pair, rs_send, rs_got, sm_part, sm_pair, sm_send, sm_got, ph_acc, fin,
     in_sem, f_s, f_r, q_s, q_r, l_s, l_r, st_s, st_r, qp_s, qp_r, qy_s, qy_r, b_s, b_r,
-    wp_s, wp_r, w_s, w_r, h_s, h_r, a_s, a_r,
+    wp_s, wp_r, w_s, w_r, hp_s, hp_r, h_s, h_r, rw_s, rw_r, a_s, a_r,
 ):
     g = lax.axis_index("group")
     r = lax.axis_index("rep")
@@ -137,10 +138,10 @@
         gg = (g + 1 + k) % 8
         at = pl.multiple_of(gg * 128, 128)
         here = pl.ds(at, 128)
-        i_hot, i_mid, i_cold = [to_col(served[pl.ds(n, 1), here]) for n in range(3)]
-        hot = mm(picks(i_hot, (128, 1024), 1).astype(BF), v_hot[...]).astype(BF)
-        rows_hot[here, :] = hot
-        near = mm(hot, v_ph[...])
+        i_hot, i_mid, i_cold = [to_col(served[n, :, here]) for n in range(3)]
+        hot = mm(picks(i_hot, (128, 1024), 1).astype(BF), v_hot[...])
+        rows_hot[pl.ds(gg * 16, 16)] = tiled(hot).astype(BF)
+        near = mm(hot.astype(BF), v_ph[...])
         mid = halves(i_mid, v_mid)
         line = halves(i_cold // 4, v_cold)
         line = jnp.where(i_cold % 4 == lane_seg, line, 0.0)
@@ -176,6 +177,12 @@
     for k in range(1, 4):
         from_y = ((y + k) % 4) * 2 + c
         ship(q_all.at[from_y], q_all.at[from_y], q_s, q_r.at[2], mate, r).start()
+
+    def send_raw(pg, pr):
+        ship(rows_hot.at[pg * 16 + pr], raw_hot.at[me], rw_s, rw_r, pg, pr).start()
+
+    all_peers(send_raw)
+    raw_hot[me] = rows_hot[me]
 
     ship(send.at[pl.ds(0, 127)], got.at[pl.ds(0, 127)], f_s, f_r, g, r).wait_recv()
 
@@ -308,44 +315,6 @@
 
     lax.fori_loop(0, 4, backward, 0)
 
-    def send_back(t):
-        cc = (t + y) % 4
-
-        def one(j, carry):
-            to = cc * 32 + (j + r + 16 * c) % 32
-
-            @pl.when(to != me)
-            def _():
-                ship(back_send.at[to], back_ref.at[me], b_s, b_r, to // 16, to % 16).start()
-
-            return carry
-
-        lax.fori_loop(0, 32, one, 0)
-
-    def slots(t, carry):
-        cc = (t + y) % 4
-        at = pl.multiple_of(cc * 256, 256)
-        slab = pl.ds(cc * 32, 32)
-        hot = mm(use_t[pl.ds(at, 256), :], pool_g[...])
-        mid = mm(use_t[pl.ds(1024 + at, 256), :], pool_g[...])
-        cold = mm(use_t[pl.ds(2048 + at, 256), :], pool_g[...])
-        sg_t[:, pl.ds(at, 256)] = mid.T.astype(BF)
-        sg_t[:, pl.ds(1024 + at, 256)] = cold.T.astype(BF)
-        b_mid = mm_nt(mid.astype(BF), p_mid[...])
-        b_cold = mm_nt(cold.astype(BF), p_cold[...])
-        for n, part in enumerate((hot[:, :128], hot[:, 128:], b_mid, b_cold)):
-            back_send[slab, n] = tiled(part).astype(BF)
-
-        @pl.when(t > 0)
-        def _():
-            send_back(t - 1)
-
-        return carry
-
-    lax.fori_loop(0, 4, slots, 0)
-    send_back(3)
-    back_ref[me] = back_send[me]
-
     def weights(i, carry):
         at = pl.multiple_of(i * 256, 256)
         first = mm(pooled_t[...], pre_g[:, pl.ds(at, 256)]).T
@@ -361,50 +330,96 @@
         return carry
 
     lax.fori_loop(0, 4, weights, 0)
+
+    pair = ship(rs_part.at[1 - c], rs_pair, wp_s, wp_r, mate, r)
+    pair.start()
+
+    def send_back(t):
+        cc = (t + y) % 4
+
+        def one(j, carry):
+            to = cc * 32 + (j + r + 16 * c) % 32
+
+            @pl.when(to != me)
+            def _():
+                ship(back_send.at[to], back_ref.at[me], b_s, b_r, to // 16, to % 16).start()
+
+            return carry
+
+        lax.fori_loop(0, 32, one, 0)
+
+    def slots(t, carry):
+        cc = (t + y) % 4
+        at = pl.multiple_of(cc * 256, 256)
+        slab = pl.ds(cc * 32, 32)
+        hot = mm(use_t[pl.ds(at, 256), :], pool_g[...])
+        mid = mm(use_t[pl.ds(1024 + at, 256), :], pool_g[...])
+        cold = mm(use_t[pl.ds(2048 + at, 256), :], pool_g[...])
+        for n, part in enumerate((hot, mid, cold)):
+            sg_t[:, pl.ds(n * 1024 + at, 256)] = part.T.astype(BF)
+        b_mid = mm_nt(mid.astype(BF), p_mid[...])
+        b_cold = mm_nt(cold.astype(BF), p_cold[...])
+        for n, part in enumerate((hot[:, :128], hot[:, 128:], b_mid, b_cold)):
+            back_send[slab, n] = tiled(part).astype(BF)
+
+        @pl.when(t > 0)
+        def _():
+            send_back(t - 1)
+
+        return carry
+
+    lax.fori_loop(0, 4, slots, 0)
+    send_back(3)
+    back_ref[me] = back_send[me]
+
+    ship(rows_hot.at[pl.ds(0, 127)], raw_hot.at[pl.ds(0, 127)], rw_s, rw_r, g, r).wait_recv()
+    ph_acc[...] = jnp.zeros_like(ph_acc)
+
+    def hot_weights(i, carry):
+        at = pl.multiple_of(i * 256, 256)
+        own = raw_hot[pl.ds(i * 32, 32)].astype(F32).reshape(256, 512).astype(BF)
+        ph_acc[...] += mm(sg_t[:, pl.ds(at, 256)], own)
+        return carry
+
+    lax.fori_loop(0, 4, hot_weights, 0)
     small = [
-        mm(sg_t[:, :1024], raw_mid[...]).reshape(16, 2, 8, 128).astype(BF),
-        mm(sg_t[:, 1024:], raw_cold[...]).reshape(16, 2, 8, 128).astype(BF),
+        mm(sg_t[:, 1024:2048], raw_mid[...]).reshape(16, 2, 8, 128).astype(BF),
+        mm(sg_t[:, 2048:], raw_cold[...]).reshape(16, 2, 8, 128).astype(BF),
     ]
     for n in range(8):
-        rs_part[n % 2, :, n // 2, 4] = small[(n // 2) % 2][:, n % 2]
-    ship(rs_part.at[1 - c], rs_pair, wp_s, wp_r, mate, r).start()
-    ship(rs_part.at[1 - c], rs_pair, wp_s, wp_r, mate, r).wait()
+        lanes = slice(128 * (n // 2), 128 * (n // 2) + 128)
+        part = ph_acc[:, lanes].reshape(16, 2, 8, 128).astype(BF)
+        sm_part[n % 2, :, n // 2, 0] = small[(n // 2) % 2][:, n % 2]
+        sm_part[n % 2, :, n // 2, 1] = part[:, n % 2]
+    small_pair = ship(sm_part.at[1 - c], sm_pair, hp_s, hp_r, mate, r)
+    small_pair.start()
+    pair.wait()
+    src = r * 4 + y
 
     def add_pair(k, carry):
         rs_send[k] = (rs_part[c, k].astype(F32) + rs_pair[k].astype(F32)).astype(BF)
         return carry
 
     lax.fori_loop(0, 16, add_pair, 0)
-    src = r * 4 + y
 
     def send_block(pg, pr):
         ship(rs_send.at[pr, pg // 2], rs_got.at[src], w_s, w_r, pg, pr).start()
 
     all_peers(send_block, 2)
     rs_got[src] = rs_send[r, y]
-    ship(back_send.at[pl.ds(0, 127)], back_ref.at[pl.ds(0, 127)], b_s, b_r, g, r).wait_recv()
-    ph_acc[...] = jnp.zeros_like(ph_acc)
-
-    def hot_weights(i, carry):
-        slab = pl.ds(i * 32, 32)
-        left = back_ref[slab, 0].astype(F32).reshape(256, 128).T.astype(BF)
-        right = back_ref[slab, 1].astype(F32).reshape(256, 128).T.astype(BF)
-        own = rows_hot[pl.ds(pl.multiple_of(i * 256, 256), 256), :]
-        ph_acc[0:128, :] += mm(left, own)
-        ph_acc[128:256, :] += mm(right, own)
-        return carry
-
-    lax.fori_loop(0, 4, hot_weights, 0)
-    for n in range(4):
-        part = ph_acc[:, 128 * n : 128 * n + 128].reshape(16, 2, 8, 128).astype(BF)
-        ph_send[:, 2 * n] = part[:, 0]
-        ph_send[:, 2 * n + 1] = part[:, 1]
-
-    def send_hot(pg, pr):
-        ship(ph_send.at[pr, pg], ph_got.at[me], h_s, h_r, pg, pr).start()
-
-    all_peers(send_hot)
-    ph_got[me] = ph_send[r, g]
+    small_pair.wait()
+
+    def add_small(k, carry):
+        sm_send[k] = (sm_part[c, k].astype(F32) + sm_pair[k].astype(F32)).astype(BF)
+        return carry
+
+    lax.fori_loop(0, 16, add_small, 0)
+
+    def send_small(pg, pr):
+        ship(sm_send.at[pr, pg // 2], sm_got.at[src], h_s, h_r, pg, pr).start()
+
+    all_peers(send_small, 2)
+    sm_got[src] = sm_send[r, y]
 
     ship(q_sum.at[pl.ds(0, 3)], q_recv, qy_s, qy_r, g, r).wait_recv()
     qg = q_sum[3].astype(F32)
@@ -417,17 +432,18 @@
     def add(k, total):
         return total + rs_got[k].astype(F32)
 
-    fin[g, pl.ds(0, 5)] = lax.fori_loop(0, 64, add, jnp.zeros((5, 8, 128), F32))
-    ship(ph_got.at[pl.ds(0, 127)], ph_got.at[pl.ds(0, 127)], h_s, h_r, g, r).wait_recv()
-
-    def add_hot(k, total):
-        return total + ph_got[k].astype(F32)
-
-    fin[g, 5] = lax.fori_loop(0, 128, add_hot, jnp.zeros((8, 128), F32))
+    fin[g, pl.ds(0, 4)] = lax.fori_loop(0, 64, add, jnp.zeros((4, 8, 128), F32))
+    ship(sm_got.at[pl.ds(0, 63)], sm_got.at[pl.ds(0, 63)], h_s, h_r, g, r).wait_recv()
+
+    def add_rest(k, total):
+        return total + sm_got[k].astype(F32)
+
+    fin[g, pl.ds(4, 2)] = lax.fori_loop(0, 64, add_rest, jnp.zeros((2, 8, 128), F32))
     for k in range(1, 8):
         ship(fin.at[g], fin.at[g], a_s, a_r, (g + k) % 8, r).start()
     ship(fin.at[pl.ds(0, 7)], fin.at[pl.ds(0, 7)], a_s, a_r, g, r).wait()
     fin_ref[...] = fin[...]
+    ship(back_send.at[pl.ds(0, 127)], back_ref.at[pl.ds(0, 127)], b_s, b_r, g, r).wait_recv()
 
     ship(send.at[pl.ds(0, 127)], got.at[pl.ds(0, 127)], f_s, f_r, g, r).wait_send()
     ship(q_all.at[pl.ds(0, 7)], q_all.at[pl.ds(0, 7)], q_s, q_r.at[0], g, r).wait_send()
@@ -438,7 +454,8 @@
     ship(q_sum.at[pl.ds(0, 3)], q_recv, qy_s, qy_r, g, r).wait_send()
     ship(back_send.at[pl.ds(0, 127)], back_ref.at[pl.ds(0, 127)], b_s, b_r, g, r).wait_send()
     ship(rs_got.at[pl.ds(0, 63)], rs_got.at[pl.ds(0, 63)], w_s, w_r, g, r).wait_send()
-    ship(ph_got.at[pl.ds(0, 127)], ph_got.at[pl.ds(0, 127)], h_s, h_r, g, r).wait_send()
+    ship(sm_got.at[pl.ds(0, 63)], sm_got.at[pl.ds(0, 63)], h_s, h_r, g, r).wait_send()
+    ship(rows_hot.at[pl.ds(0, 127)], raw_hot.at[pl.ds(0, 127)], rw_s, rw_r, g, r).wait_send()
 
 
 def scatter_kernel(
@@ -459,8 +476,8 @@
                 mm_nt(flat(back[slab, 0]), p_hot[:, 0:128])
                 + mm_nt(flat(back[slab, 1]), p_hot[:, 128:256])
             ).astype(BF)
-            i_mid = to_col(served[1:2, here])
-            i_cold = to_col(served[2:3, here])
+            i_mid = to_col(served[1, :, here])
+            i_cold = to_col(served[2, :, here])
             mid = flat(back[slab, 2])
             cold = jnp.where(i_cold % 4 == lane_seg, flat(back[slab, 3]), zero)
             for n in range(2):
@@ -469,24 +486,24 @@
                 b_cold[here, lanes] = jnp.where(i_cold // 8192 == n, cold, zero)
         out_loss[...] = loss[...]
         for n in range(2):
-            o_in[128 * n : 128 * n + 128, :] = fin[:, n].reshape(64, 128).T
+            o_in[:, 128 * n : 128 * n + 128] = fin[:, n].reshape(64, 128)
         for n in range(8):
-            o_out[128 * n : 128 * n + 128, :] = fin[n, 2:4].reshape(16, 128).T
+            o_out[:, 128 * n : 128 * n + 128] = fin[n, 2:4].reshape(16, 128)
         for n in range(4):
-            o_ph[128 * n : 128 * n + 128, :] = fin[2 * n : 2 * n + 2, 5].reshape(16, 128).T
-        o_pm[...] = fin[0:2, 4].reshape(16, 128).T
-        cold_t = fin[2:4, 4].reshape(16, 128).T
-        o_pc[...] = cold_t[0:32] + cold_t[32:64] + cold_t[64:96] + cold_t[96:128]
+            o_ph[:, 128 * n : 128 * n + 128] = fin[2 * n : 2 * n + 2, 5].reshape(16, 128)
+        o_pm[...] = fin[0:2, 4].reshape(16, 128)
+        part = fin[2:4, 4].reshape(16, 128)
+        o_pc[...] = part[:, 0:32] + part[:, 32:64] + part[:, 64:96] + part[:, 96:128]
 
     out_qg[...] = qg_t[...].T
     idx = served[...]
-    hot = picks(idx[0:1] - step * 256, (256, 1024), 0).astype(BF)
+    hot = picks(idx[0] - step * 256, (256, 1024), 0).astype(BF)
     out_hot[...] = mm(hot, b_hot[...])
-    mid = picks(idx[1:2] % 2048 - step * 512, (512, 1024), 0).astype(BF)
+    mid = picks(idx[1] % 2048 - step * 512, (512, 1024), 0).astype(BF)
     both = mm(mid, b_mid[...])
     out_mid[0] = both[:, :128]
     out_mid[1] = both[:, 128:]
-    cold = picks((idx[2:3] // 4) % 2048 - step * 512, (512, 1024), 0).astype(BF)
+    cold = picks((idx[2] // 4) % 2048 - step * 512, (512, 1024), 0).astype(BF)
     both = mm(cold, b_cold[...])
     out_cold[0] = both[:, :128]
     out_cold[1] = both[:, 128:]
@@ -507,38 +524,39 @@
     item_block,
     serve_rows,
 ):
-    served = serve_rows[0]
+    served = serve_rows.transpose(1, 0, 2)
     anywhere = pl.BlockSpec(memory_space=pl.ANY)
     vmem = pl.BlockSpec(memory_space=pltpu.VMEM)
     sds = jax.ShapeDtypeStruct
     V = pltpu.VMEM
-    back, _, qg_t, loss, fin = pl.pallas_call(
+    back, qg_t, loss, fin = pl.pallas_call(
         step_kernel,
         out_shape=[
             sds((128, 4, 8, 128), BF),
-            sds((1024, 512), BF),
             sds((256, 512), F32),
             sds((1, 512), F32),
             sds((8, 6, 8, 128), F32),
         ],
         in_specs=[anywhere] * 4 + [vmem] * 2 + [anywhere] * 3 + [vmem] * 4,
-        out_specs=[vmem] * 5,
+        out_specs=[vmem] * 4,
         scratch_shapes=[
             V((1024, 512), BF), V((2048, 256), BF), V((2048, 256), BF), V((512, 256), BF),
             V((256, 1024), BF), V((1024, 256), BF), V((8, 512, 256), BF), V((8, 1, 512), jnp.int32),
-            V((128, 4, 8, 128), BF), V((128, 4, 8, 128), BF), V((3072, 1024), BF),
+            V((128, 4, 8, 128), BF), V((128, 4, 8, 128), BF), V((128, 8, 512), BF),
+            V((128, 8, 512), BF), V((3072, 1024), BF),
             V((256, 3072), BF), V((1024, 128), BF), V((1024, 128), BF), V((128, 256), BF),
             V((256, 128), BF), V((256, 128), BF), V((256, 1024), BF), V((1024, 1024), F32),
             V((1024, 1024), BF), V((1024, 256), F32), V((1024, 256), BF), V((256, 1024), BF),
             V((8, 8, 2, 512), F32), V((8, 1, 512), F32), V((1024, 256), F32),
             V((4, 256, 512), BF), V((4, 256, 512), BF), V((4, 256, 512), BF),
             V((3, 256, 512), BF), V((1024, 1024), BF), V((1024, 256), BF), V((256, 1024), BF),
-            V((256, 2048), BF), V((128, 4, 8, 128), BF), V((2, 16, 4, 5, 8, 128), BF),
-            V((16, 4, 5, 8, 128), BF), V((16, 4, 5, 8, 128), BF), V((64, 5, 8, 128), BF),
-            V((16, 8, 8, 128), BF), V((128, 8, 128), BF), V((256, 512), F32),
+            V((256, 3072), BF), V((128, 4, 8, 128), BF), V((2, 16, 4, 4, 8, 128), BF),
+            V((16, 4, 4, 8, 128), BF), V((16, 4, 4, 8, 128), BF), V((64, 4, 8, 128), BF),
+            V((2, 16, 4, 2, 8, 128), BF), V((16, 4, 2, 8, 128), BF), V((16, 4, 2, 8, 128), BF),
+            V((64, 2, 8, 128), BF), V((256, 512), F32),
             V((8, 6, 8, 128), F32),
             DMA((9,)), DMA, DMA, DMA, DMA((3,)), DMA, DMA, DMA, DMA((8,)), DMA, DMA((4,)),
-            DMA, DMA, DMA, DMA, DMA, DMA, DMA, DMA, DMA, DMA, DMA, DMA,
+            DMA, DMA, DMA, DMA, DMA, DMA, DMA, DMA, DMA, DMA, DMA, DMA, DMA, DMA, DMA, DMA,
         ],
         compiler_params=pltpu.CompilerParams(
             collective_id=1, has_side_effects=True, vmem_limit_bytes=63 << 20
@@ -551,8 +569,8 @@
     full = lambda a: pl.BlockSpec(a.shape, lambda i: (0,) * a.ndim)
     outs = [
         sds((1024, 512), F32), sds((2, 2048, 128), F32), sds((2, 2048, 128), F32),
-        sds((512, 256), F32), sds((1, 512), F32), sds((512, 16), F32), sds((128, 16), F32),
-        sds((32, 16), F32), sds((256, 64), F32), sds((1024, 16), F32),
+        sds((512, 256), F32), sds((1, 512), F32), sds((16, 512), F32), sds((16, 128), F32),
+        sds((16, 32), F32), sds((64, 256), F32), sds((16, 1024), F32),
     ]
     grad_hot, grad_mid, grad_cold, query_grad, query_loss, *rest = pl.pallas_call(
         scatter_kernel,
@@ -571,7 +589,7 @@
         out_shape=outs,
         scratch_shapes=[V((1024, 512), BF), V((1024, 256), BF), V((1024, 256), BF)],
         compiler_params=pltpu.CompilerParams(
-            dimension_semantics=("arbitrary",), vmem_limit_bytes=40 << 20
+            dimension_semantics=("arbitrary",), vmem_limit_bytes=63 << 20
         ),
         name="scatter",
     )(back, served, proj_hot, fin, qg_t, loss)
@@ -581,7 +599,7 @@
         grad_hot,
         grad_mid.reshape(4096, 128),
         grad_cold.reshape(4096, 128),
-        *rest,
+        *[v.T for v in rest],
     )
 
 

time: 130 us -> 117 us (0.900)
  local copies, waits for them, and re-layouts: 8.71 us -> 0 us
  Pallas kernels: 120 us -> 116 us
    unnamed x18 -> x0, local copies, waits for them, and re-layouts: 8.71 us -> none
    pallas_call x1, Pallas kernels: 113 us -> 108 us  [local(): pl.pallas_call(step_kernel, out_shape=[sds((128, 4, 8, 128), BF), sds((25...]
where the time goes in v2:
time: 117 us
  Pallas kernels  116 us (99%)
    pallas_call x1, Pallas kernels, local(): pl.pallas_call(step_kernel, out_shape=[sds((128, 4, 8, 128), BF), sds((25...  108 us
    pallas_call x1, Pallas kernels, local(): pl.pallas_call(scatter_kernel, grid=(4,), in_specs=[full(back), full(serv...  8.33 us

profile of v2, /device:TPU:1, one launch (start us, length us, event | category | flops | bytes accessed | tf_op | source)
XLA Modules:
  0.0 116.9 jit_solution(2250363211831126915)
XLA Ops:
  0.6 107.9 %step.1 = (bf16[128,4,8,128]{3,2,1,0:T(8,128)(2,1)}, f32[256,512]{1,0:T(8,128)}, f32[1,512]{1,0:T(1,128)}, f32[8,6,8,128]{3,2,1,0:T(8,128)}) custom-call(bf16[1024,512]{1,0:T(8,128)(2,1)} %t_hot.1, bf16[4096,128]{1,0:T(8,128)(2,1)} %t_mid.1, bf16[4096,128]{1,0:T(8,128)(2,1)} %t_cold.1, bf16[512,256]{1,0:T(8,128)(2,1)} %p_hot.3, bf16[128,256]{1,0:T(8,128)(2,1)} %p_mid.1, ...), custom_call_target="tpu_custom_call" | custom-call | tf_op jit(solution)/shard_map/step/pallas_call | solution.py:532
  108.6 8.3 %scatter.1 = (f32[1024,512]{1,0:T(8,128)}, f32[2,2048,128]{2,1,0:T(8,128)}, f32[2,2048,128]{2,1,0:T(8,128)}, f32[512,256]{1,0:T(8,128)}, f32[1,512]{1,0:T(1,128)...) custom-call(bf16[128,4,8,128]{3,2,1,0:T(8,128)(2,1)} %get-tuple-elem, ...), custom_call_target="tpu_custom_call" | custom-call | tf_op jit(solution)/shard_map/scatter/pallas_call | solution.py:575

commit v3 on v2

--- a/solution.py
+++ b/solution.py
@@ -51,12 +51,11 @@
     t_hot, t_mid, t_cold, p_hot, p_mid, proj_cold, w_in, w_out, queries, labels, served,
     item_slot, item_block,
     back_ref, qg_out, loss_out, fin_ref,
-    v_hot, v_mid, v_cold, v_ph, v_in, v_out, q_all, lab_all, send, got, rows_hot,
-    raw_hot, use_t, slot_t,
+    v_hot, v_mid, v_cold, v_ph, v_in, v_out, q_all, lab_all, send, got, rows_hot, use_t, slot_t,
     raw_mid, raw_cold, p_cold, p_mid_t, p_cold_t, pooled_t, pre, hidden, resid, vec, vec_t, stat, loss_all, vg,
-    q_send, q_part, q_sum, q_recv, pre_g, pool_g, low_t, sg_t, back_send, rs_part,
-    rs_pair, rs_send, rs_got, sm_part, sm_pair, sm_send, sm_got, ph_acc, fin,
-    in_sem, f_s, f_r, q_s, q_r, l_s, l_r, st_s, st_r, qp_s, qp_r, qy_s, qy_r, b_s, b_r,
+    q_send, q_part, q_sum, q_recv, q_half, pre_g, pool_g, low_t, sg_t, back_send, rs_part,
+    rs_pair, rs_send, rs_got, sm_part, sm_pair, ph_send, ph_got, ph_acc, fin, shares,
+    in_sem, f_s, f_r, q_s, q_r, l_s, l_r, st_s, st_r, qp_s, qp_r, qy_s, qy_r, qh_r, b_s, b_r,
     wp_s, wp_r, w_s, w_r, hp_s, hp_r, h_s, h_r, rw_s, rw_r, a_s, a_r,
 ):
     g = lax.axis_index("group")
@@ -73,7 +72,7 @@
                 visit(pg, lax.rem(r + j, 16))
                 return carry
 
-            lax.fori_loop(0 if k else 1, 16, one, 0)
+            lax.fori_loop(0 if k else 1, 16, one, 0, unroll=4 if k else 5)
 
     def ship(src, dst, s_sem, r_sem, pg, pr):
         return pltpu.make_async_remote_copy(
@@ -140,8 +139,9 @@
         here = pl.ds(at, 128)
         i_hot, i_mid, i_cold = [to_col(served[n, :, here]) for n in range(3)]
         hot = mm(picks(i_hot, (128, 1024), 1).astype(BF), v_hot[...])
-        rows_hot[pl.ds(gg * 16, 16)] = tiled(hot).astype(BF)
-        near = mm(hot.astype(BF), v_ph[...])
+        hot = hot.astype(BF)
+        rows_hot[here, :] = hot
+        near = mm(hot, v_ph[...])
         mid = halves(i_mid, v_mid)
         line = halves(i_cold // 4, v_cold)
         line = jnp.where(i_cold % 4 == lane_seg, line, 0.0)
@@ -155,8 +155,10 @@
         send_rows(k)
     got[me] = send[me]
     held[6].wait()
-    for k in range(1, 4):
-        ship(q_all.at[g], q_all.at[g], q_s, q_r.at[0], ((y + k) % 4) * 2 + c, r).start()
+    up, down, far = [((y + k) % 4) * 2 + c for k in (1, 3, 2)]
+    top_half, low_half = pl.ds(0, 256), pl.ds(256, 256)
+    ship(q_all.at[g], q_all.at[g], q_s, q_r.at[0], up, r).start()
+    ship(q_all.at[g], q_all.at[g], q_s, q_r.at[3], down, r).start()
     ship(q_all.at[g], q_all.at[g], q_s, q_r.at[1], mate, r).start()
     for k in range(1, 8):
         ship(lab_all.at[g], lab_all.at[g], l_s, l_r, (g + k) % 8, r).start()
@@ -173,17 +175,6 @@
         return carry
 
     lax.fori_loop(0, 12, count_slots, 0)
-    ship(q_all.at[pl.ds(0, 3)], q_all.at[pl.ds(0, 3)], q_s, q_r.at[0], g, r).wait_recv()
-    for k in range(1, 4):
-        from_y = ((y + k) % 4) * 2 + c
-        ship(q_all.at[from_y], q_all.at[from_y], q_s, q_r.at[2], mate, r).start()
-
-    def send_raw(pg, pr):
-        ship(rows_hot.at[pg * 16 + pr], raw_hot.at[me], rw_s, rw_r, pg, pr).start()
-
-    all_peers(send_raw)
-    raw_hot[me] = rows_hot[me]
-
     ship(send.at[pl.ds(0, 127)], got.at[pl.ds(0, 127)], f_s, f_r, g, r).wait_recv()
 
     def fill(i, carry):
@@ -223,7 +214,21 @@
         vec_t[:, here] = v.T.astype(BF)
         return carry
 
-    lax.fori_loop(0, 4, forward, 0)
+    lax.fori_loop(0, 2, forward, 0)
+
+    def onto_mate(block):
+        ship(q_all.at[block], q_all.at[block], q_s, q_r.at[2], mate, r).start()
+
+    ship(q_all.at[g], q_all.at[g], q_s, q_r.at[0], up, r).wait_recv()
+    ship(q_all.at[down, top_half], q_all.at[down, top_half], q_s, q_r.at[4], up, r).start()
+    onto_mate(down)
+    ship(q_all.at[g], q_all.at[g], q_s, q_r.at[3], down, r).wait_recv()
+    ship(q_all.at[up, low_half], q_all.at[up, low_half], q_s, q_r.at[4], down, r).start()
+    onto_mate(up)
+
+    lax.fori_loop(2, 4, forward, 0)
+    ship(q_all.at[far], q_all.at[far], q_s, q_r.at[4], up, r).wait_recv()
+    onto_mate(far)
 
     ship(q_all.at[g], q_all.at[g], q_s, q_r.at[1], mate, r).wait_recv()
     ship(q_all.at[pl.ds(0, 3)], q_all.at[pl.ds(0, 3)], q_s, q_r.at[2], g, r).wait_recv()
@@ -281,15 +286,30 @@
 
     lax.fori_loop(0, 4, for_mate, 0)
 
-    def for_self(i, carry):
-        at_y = (y + 1 + i) % 4
-        mine = grads(at_y * 2 + c)
+    halves_of = (pl.ds(0, 128), pl.ds(128, 128))
+
+    def for_self(t, carry):
+        i = t + (1 - 2 * t) * (1 - t // 2)
+        mine = grads(((y + 1 + i) % 4) * 2 + c)
         ship(q_send.at[i], q_part.at[i], qp_s, qp_r.at[i], mate, r).wait_recv()
-        q_sum[i] = (mine + q_part[i].astype(F32)).astype(BF)
-
-        @pl.when(i < 3)
+        total = mine + q_part[i].astype(F32)
+        q_sum[i] = total.astype(BF)
+
+        @pl.when(t == 0)
         def _():
-            ship(q_sum.at[i], q_recv.at[i], qy_s, qy_r, at_y * 2 + c, r).start()
+            for n, to in enumerate((up, down)):
+                part = halves_of[n]
+                ship(q_sum.at[1, part], q_half.at[n], qy_s, qh_r.at[n], to, r).start()
+
+        for n, to in enumerate((up, down)):
+
+            @pl.when(t == n + 1)
+            def _(n=n, to=to):
+                part = halves_of[n]
+                ship(q_sum.at[1, part], q_half.at[n], qy_s, qh_r.at[n], to, r).wait_recv()
+                more = total[128 * n : 128 * n + 128] + q_half[n].astype(F32)
+                q_sum[2 * n, part] = more.astype(BF)
+                ship(q_sum.at[2 * n], q_recv.at[n], qy_s, qy_r, to, r).start()
 
         return carry
 
@@ -355,7 +375,7 @@
         hot = mm(use_t[pl.ds(at, 256), :], pool_g[...])
         mid = mm(use_t[pl.ds(1024 + at, 256), :], pool_g[...])
         cold = mm(use_t[pl.ds(2048 + at, 256), :], pool_g[...])
-        for n, part in enumerate((hot, mid, cold)):
+        for n, part in enumerate((mid, cold)):
             sg_t[:, pl.ds(n * 1024 + at, 256)] = part.T.astype(BF)
         b_mid = mm_nt(mid.astype(BF), p_mid[...])
         b_cold = mm_nt(cold.astype(BF), p_cold[...])
@@ -372,58 +392,65 @@
     send_back(3)
     back_ref[me] = back_send[me]
 
-    ship(rows_hot.at[pl.ds(0, 127)], raw_hot.at[pl.ds(0, 127)], rw_s, rw_r, g, r).wait_recv()
-    ph_acc[...] = jnp.zeros_like(ph_acc)
-
-    def hot_weights(i, carry):
-        at = pl.multiple_of(i * 256, 256)
-        own = raw_hot[pl.ds(i * 32, 32)].astype(F32).reshape(256, 512).astype(BF)
-        ph_acc[...] += mm(sg_t[:, pl.ds(at, 256)], own)
-        return carry
-
-    lax.fori_loop(0, 4, hot_weights, 0)
     small = [
-        mm(sg_t[:, 1024:2048], raw_mid[...]).reshape(16, 2, 8, 128).astype(BF),
-        mm(sg_t[:, 2048:], raw_cold[...]).reshape(16, 2, 8, 128).astype(BF),
+        mm(sg_t[:, :1024], raw_mid[...]).reshape(16, 2, 8, 128).astype(BF),
+        mm(sg_t[:, 1024:], raw_cold[...]).reshape(16, 2, 8, 128).astype(BF),
     ]
     for n in range(8):
-        lanes = slice(128 * (n // 2), 128 * (n // 2) + 128)
-        part = ph_acc[:, lanes].reshape(16, 2, 8, 128).astype(BF)
-        sm_part[n % 2, :, n // 2, 0] = small[(n // 2) % 2][:, n % 2]
-        sm_part[n % 2, :, n // 2, 1] = part[:, n % 2]
+        sm_part[n % 2, :, n // 2] = small[(n // 2) % 2][:, n % 2]
     small_pair = ship(sm_part.at[1 - c], sm_pair, hp_s, hp_r, mate, r)
     small_pair.start()
     pair.wait()
     src = r * 4 + y
 
     def add_pair(k, carry):
-        rs_send[k] = (rs_part[c, k].astype(F32) + rs_pair[k].astype(F32)).astype(BF)
+        total = rs_part[c, k].astype(F32) + rs_pair[k].astype(F32)
+        rs_send[k, :, pl.ds(0, 4)] = total.astype(BF)
         return carry
 
     lax.fori_loop(0, 16, add_pair, 0)
+    small_pair.wait()
+
+    def add_small(k, carry):
+        rs_send[k, :, 4] = (sm_part[c, k].astype(F32) + sm_pair[k].astype(F32)).astype(BF)
+        return carry
+
+    lax.fori_loop(0, 16, add_small, 0)
 
     def send_block(pg, pr):
         ship(rs_send.at[pr, pg // 2], rs_got.at[src], w_s, w_r, pg, pr).start()
 
     all_peers(send_block, 2)
     rs_got[src] = rs_send[r, y]
-    small_pair.wait()
-
-    def add_small(k, carry):
-        sm_send[k] = (sm_part[c, k].astype(F32) + sm_pair[k].astype(F32)).astype(BF)
-        return carry
-
-    lax.fori_loop(0, 16, add_small, 0)
-
-    def send_small(pg, pr):
-        ship(sm_send.at[pr, pg // 2], sm_got.at[src], h_s, h_r, pg, pr).start()
-
-    all_peers(send_small, 2)
-    sm_got[src] = sm_send[r, y]
-
-    ship(q_sum.at[pl.ds(0, 3)], q_recv, qy_s, qy_r, g, r).wait_recv()
+
+    ship(back_send.at[pl.ds(0, 127)], back_ref.at[pl.ds(0, 127)], b_s, b_r, g, r).wait_recv()
+    ph_acc[...] = jnp.zeros_like(ph_acc)
+
+    def hot_weights(i, carry):
+        slab = pl.ds(i * 32, 32)
+        own = rows_hot[pl.ds(pl.multiple_of(i * 256, 256), 256), :]
+        for n in range(2):
+            turned = back_ref[slab, n].astype(F32).reshape(256, 128).T.astype(BF)
+            ph_acc[pl.ds(128 * n, 128), :] += mm(turned, own)
+        return carry
+
+    lax.fori_loop(0, 4, hot_weights, 0)
+    for n in range(8):
+        lanes = slice(128 * (n // 2), 128 * (n // 2) + 128)
+        part = ph_acc[:, lanes].reshape(16, 2, 8, 128).astype(BF)
+        ph_send[:, n] = part[:, n % 2]
+
+    def send_hot(j, carry):
+        pr = lax.rem(r + j, 16)
+        ship(ph_send.at[pr], ph_got.at[r], rw_s, rw_r, g, pr).start()
+        return carry
+
+    lax.fori_loop(1, 16, send_hot, 0)
+    ph_got[r] = ph_send[r]
+
+    ship(q_sum.at[pl.ds(0, 2)], q_recv, qy_s, qy_r, g, r).wait_recv()
     qg = q_sum[3].astype(F32)
-    for n in range(3):
+    for n in range(2):
         qg += q_recv[n].astype(F32)
     qg_out[...] = qg
 
@@ -432,18 +459,23 @@
     def add(k, total):
         return total + rs_got[k].astype(F32)
 
-    fin[g, pl.ds(0, 4)] = lax.fori_loop(0, 64, add, jnp.zeros((4, 8, 128), F32))
-    ship(sm_got.at[pl.ds(0, 63)], sm_got.at[pl.ds(0, 63)], h_s, h_r, g, r).wait_recv()
-
-    def add_rest(k, total):
-        return total + sm_got[k].astype(F32)
-
-    fin[g, pl.ds(4, 2)] = lax.fori_loop(0, 64, add_rest, jnp.zeros((2, 8, 128), F32))
+    fin[g] = lax.fori_loop(0, 64, add, jnp.zeros((5, 8, 128), F32))
     for k in range(1, 8):
         ship(fin.at[g], fin.at[g], a_s, a_r, (g + k) % 8, r).start()
+    ship(ph_got.at[pl.ds(0, 15)], ph_got.at[pl.ds(0, 15)], rw_s, rw_r, g, r).wait_recv()
+
+    def add_hot(k, total):
+        return total + ph_got[k].astype(F32)
+
+    shares[g] = lax.fori_loop(0, 16, add_hot, jnp.zeros((8, 8, 128), F32)).astype(BF)
+    for k in range(1, 8):
+        ship(shares.at[g], shares.at[g], h_s, h_r, (g + k) % 8, r).start()
     ship(fin.at[pl.ds(0, 7)], fin.at[pl.ds(0, 7)], a_s, a_r, g, r).wait()
-    fin_ref[...] = fin[...]
-    ship(back_send.at[pl.ds(0, 127)], back_ref.at[pl.ds(0, 127)], b_s, b_r, g, r).wait_recv()
+    ship(shares.at[pl.ds(0, 7)], shares.at[pl.ds(0, 7)], h_s, h_r, g, r).wait()
+    for n in range(8):
+        fin_ref[n, pl.ds(0, 5)] = fin[n]
+        parts = [shares[k, n].astype(F32) for k in range(8)]
+        fin_ref[n, 5] = functools.reduce(jnp.add, parts)
 
     ship(send.at[pl.ds(0, 127)], got.at[pl.ds(0, 127)], f_s, f_r, g, r).wait_send()
     ship(q_all.at[pl.ds(0, 7)], q_all.at[pl.ds(0, 7)], q_s, q_r.at[0], g, r).wait_send()
@@ -451,11 +483,10 @@
     for b in range(8):
         ship(stat.at[b, pl.ds(0, 7)], stat.at[b, pl.ds(0, 7)], st_s, st_r.at[0], g, r).wait_send()
     ship(q_send, q_part, qp_s, qp_r.at[0], g, r).wait_send()
-    ship(q_sum.at[pl.ds(0, 3)], q_recv, qy_s, qy_r, g, r).wait_send()
+    ship(q_sum.at[pl.ds(0, 3)], q_sum.at[pl.ds(0, 3)], qy_s, qy_r, g, r).wait_send()
     ship(back_send.at[pl.ds(0, 127)], back_ref.at[pl.ds(0, 127)], b_s, b_r, g, r).wait_send()
     ship(rs_got.at[pl.ds(0, 63)], rs_got.at[pl.ds(0, 63)], w_s, w_r, g, r).wait_send()
-    ship(sm_got.at[pl.ds(0, 63)], sm_got.at[pl.ds(0, 63)], h_s, h_r, g, r).wait_send()
-    ship(rows_hot.at[pl.ds(0, 127)], raw_hot.at[pl.ds(0, 127)], rw_s, rw_r, g, r).wait_send()
+    ship(ph_got.at[pl.ds(0, 15)], ph_got.at[pl.ds(0, 15)], rw_s, rw_r, g, r).wait_send()
 
 
 def scatter_kernel(
@@ -542,21 +573,21 @@
         scratch_shapes=[
             V((1024, 512), BF), V((2048, 256), BF), V((2048, 256), BF), V((512, 256), BF),
             V((256, 1024), BF), V((1024, 256), BF), V((8, 512, 256), BF), V((8, 1, 512), jnp.int32),
-            V((128, 4, 8, 128), BF), V((128, 4, 8, 128), BF), V((128, 8, 512), BF),
-            V((128, 8, 512), BF), V((3072, 1024), BF),
+            V((128, 4, 8, 128), BF), V((128, 4, 8, 128), BF), V((1024, 512), BF),
+            V((3072, 1024), BF),
             V((256, 3072), BF), V((1024, 128), BF), V((1024, 128), BF), V((128, 256), BF),
             V((256, 128), BF), V((256, 128), BF), V((256, 1024), BF), V((1024, 1024), F32),
             V((1024, 1024), BF), V((1024, 256), F32), V((1024, 256), BF), V((256, 1024), BF),
             V((8, 8, 2, 512), F32), V((8, 1, 512), F32), V((1024, 256), F32),
             V((4, 256, 512), BF), V((4, 256, 512), BF), V((4, 256, 512), BF),
-            V((3, 256, 512), BF), V((1024, 1024), BF), V((1024, 256), BF), V((256, 1024), BF),
-            V((256, 3072), BF), V((128, 4, 8, 128), BF), V((2, 16, 4, 4, 8, 128), BF),
-            V((16, 4, 4, 8, 128), BF), V((16, 4, 4, 8, 128), BF), V((64, 4, 8, 128), BF),
-            V((2, 16, 4, 2, 8, 128), BF), V((16, 4, 2, 8, 128), BF), V((16, 4, 2, 8, 128), BF),
-            V((64, 2, 8, 128), BF), V((256, 512), F32),
-            V((8, 6, 8, 128), F32),
-            DMA((9,)), DMA, DMA, DMA, DMA((3,)), DMA, DMA, DMA, DMA((8,)), DMA, DMA((4,)),
-            DMA, DMA, DMA, DMA, DMA, DMA, DMA, DMA, DMA, DMA, DMA, DMA, DMA, DMA, DMA, DMA,
+            V((2, 256, 512), BF), V((2, 128, 512), BF), V((1024, 1024), BF), V((1024, 256), BF), V((256, 1024), BF),
+            V((256, 2048), BF), V((128, 4, 8, 128), BF), V((2, 16, 4, 4, 8, 128), BF),
+            V((16, 4, 4, 8, 128), BF), V((16, 4, 5, 8, 128), BF), V((64, 5, 8, 128), BF),
+            V((2, 16, 4, 8, 128), BF), V((16, 4, 8, 128), BF), V((16, 8, 8, 128), BF),
+            V((16, 8, 8, 128), BF), V((256, 512), F32), V((8, 5, 8, 128), F32),
+            V((8, 8, 8, 128), BF),
+            DMA((9,)), DMA, DMA, DMA, DMA((5,)), DMA, DMA, DMA, DMA((8,)), DMA, DMA((4,)),
+            DMA, DMA, DMA((2,)), DMA, DMA, DMA, DMA, DMA, DMA, DMA, DMA, DMA, DMA, DMA, DMA, DMA, DMA,
         ],
         compiler_params=pltpu.CompilerParams(
             collective_id=1, has_side_effects=True, vmem_limit_bytes=63 << 20

time: 117 us -> 115 us (0.983)
  Pallas kernels: 116 us -> 114 us
    pallas_call x1, Pallas kernels: 108 us -> 106 us  [local(): pl.pallas_call(step_kernel, out_shape=[sds((128, 4, 8, 128), BF), sds((25...]
where the time goes in v3:
time: 115 us
  Pallas kernels  114 us (99%)
    pallas_call x1, Pallas kernels, local(): pl.pallas_call(step_kernel, out_shape=[sds((128, 4, 8, 128), BF), sds((25...  106 us
    pallas_call x1, Pallas kernels, local(): pl.pallas_call(scatter_kernel, grid=(4,), in_specs=[full(back), full(serv...  8.32 us

profile of v3, /device:TPU:1, one launch (start us, length us, event | category | flops | bytes accessed | tf_op | source)
XLA Modules:
  0.0 114.6 jit_solution(5333829921932529616)
XLA Ops:
  0.6 105.6 %step.1 = (bf16[128,4,8,128]{3,2,1,0:T(8,128)(2,1)}, f32[256,512]{1,0:T(8,128)}, f32[1,512]{1,0:T(1,128)}, f32[8,6,8,128]{3,2,1,0:T(8,128)}) custom-call(bf16[1024,512]{1,0:T(8,128)(2,1)} %t_hot.1, bf16[4096,128]{1,0:T(8,128)(2,1)} %t_mid.1, bf16[4096,128]{1,0:T(8,128)(2,1)} %t_cold.1, bf16[512,256]{1,0:T(8,128)(2,1)} %p_hot.3, bf16[128,256]{1,0:T(8,128)(2,1)} %p_mid.1, ...), custom_call_target="tpu_custom_call" | custom-call | tf_op jit(solution)/shard_map/step/pallas_call | solution.py:563
  106.3 8.3 %scatter.1 = (f32[1024,512]{1,0:T(8,128)}, f32[2,2048,128]{2,1,0:T(8,128)}, f32[2,2048,128]{2,1,0:T(8,128)}, f32[512,256]{1,0:T(8,128)}, f32[1,512]{1,0:T(1,128)...) custom-call(bf16[128,4,8,128]{3,2,1,0:T(8,128)(2,1)} %get-tuple-elem, ...), custom_call_target="tpu_custom_call" | custom-call | tf_op jit(solution)/shard_map/scatter/pallas_call | solution.py:606

commit v4 on v3

--- a/solution.py
+++ b/solution.py
@@ -13,8 +13,8 @@
 F32 = jnp.float32
 BOTH = ("group", "rep")
 MESH = pl.DeviceIdType.MESH
-SCALE2 = LOGIT_SCALE * 1.4426950408889634
-LN2 = 0.6931471805599453
+LOG2E = 1.4426950408889634
+SCALE2 = LOGIT_SCALE * LOG2E
 DMA = pltpu.SemaphoreType.DMA
 
 
@@ -274,7 +274,7 @@
         loss_all[b] = joint - hits
         st = mm_nt(vec[...], q_all[b])
         hit = label_rows(b) == lax.broadcasted_iota(jnp.int32, st.shape, 0)
-        prob = jnp.exp2((st * LOGIT_SCALE - joint) * 1.4426950408889634)
+        prob = jnp.exp2(st * SCALE2 - joint * LOG2E)
         grad = (prob - jnp.where(hit, 1.0, 0.0)).astype(BF)
         vg[...] += mm(grad, q_all[b])
         return LOGIT_SCALE * mm(vec_t[...], grad)

time: 115 us -> 115 us (level)
  no operation moved by 1% of the time
where the time goes in v4:
time: 115 us
  Pallas kernels  114 us (99%)
    pallas_call x1, Pallas kernels, local(): pl.pallas_call(step_kernel, out_shape=[sds((128, 4, 8, 128), BF), sds((25...  106 us
    pallas_call x1, Pallas kernels, local(): pl.pallas_call(scatter_kernel, grid=(4,), in_specs=[full(back), full(serv...  8.33 us

profile of v4, /device:TPU:1, one launch (start us, length us, event | category | flops | bytes accessed | tf_op | source)
XLA Modules:
  0.0 115.1 jit_solution(11215640100816065124)
XLA Ops:
  0.6 106.1 %step.1 = (bf16[128,4,8,128]{3,2,1,0:T(8,128)(2,1)}, f32[256,512]{1,0:T(8,128)}, f32[1,512]{1,0:T(1,128)}, f32[8,6,8,128]{3,2,1,0:T(8,128)}) custom-call(bf16[1024,512]{1,0:T(8,128)(2,1)} %t_hot.1, bf16[4096,128]{1,0:T(8,128)(2,1)} %t_mid.1, bf16[4096,128]{1,0:T(8,128)(2,1)} %t_cold.1, bf16[512,256]{1,0:T(8,128)(2,1)} %p_hot.3, bf16[128,256]{1,0:T(8,128)(2,1)} %p_mid.1, ...), custom_call_target="tpu_custom_call" | custom-call | tf_op jit(solution)/shard_map/step/pallas_call | solution.py:563
  106.8 8.3 %scatter.1 = (f32[1024,512]{1,0:T(8,128)}, f32[2,2048,128]{2,1,0:T(8,128)}, f32[2,2048,128]{2,1,0:T(8,128)}, f32[512,256]{1,0:T(8,128)}, f32[1,512]{1,0:T(1,128)...) custom-call(bf16[128,4,8,128]{3,2,1,0:T(8,128)(2,1)} %get-tuple-elem, ...), custom_call_target="tpu_custom_call" | custom-call | tf_op jit(solution)/shard_map/scatter/pallas_call | solution.py:606
